TPU v7x, 32 devices: a whole 2x2x4 slice. The times are simulated.
32 devices in a mesh: cluster: 2 (over x), sub: 16 (over z, y, core).
Axes of the slice: x: 2, y: 2, z: 4, core: 2. Of those that a mesh axis runs over, the one named last changes fastest.
Arguments:
- load_terms: float32 [32, 128, 1536], P(('cluster', 'sub')), may hold values from -60 to 60
- dual_operator: bfloat16 [32, 1536, 1536], P(('cluster', 'sub')), may hold values from -2 to 16, as said below
- dirichlet: bfloat16 [32, 1536, 1536], P(('cluster', 'sub')), may hold values from -2 to 16, as said below
- corner_coupling: bfloat16 [32, 1536, 24], P(('cluster', 'sub')), may hold values from -0.25 to 0.25
- coarse_inverse: float32 [96, 96], P(('cluster', 'sub')), may hold values from -2 to 4, as said below
- face_map: int32 [32, 6, 256], P(('cluster', 'sub')), may hold values from 0 to 255, as said below
- face_live: int32 [32, 6], P(('cluster', 'sub')), may hold values from 0 to 1, as said below
- corner_ids: int32 [32, 8], P(('cluster', 'sub')), may hold values from 0 to 31, as said below
Outputs:
- multipliers: float32 [32, 128, 1536], P(('cluster', 'sub'))
- residual: float32 [32, 128, 1536], P(('cluster', 'sub'))
Inputs may be any that keep to these rules, and one draw needn't show every extreme that they name: face_map[d, f] is a permutation of the slots of a face; the maps of the two sides of a face pair are inverse to each other. `face_live`: equal on the two sides of a face pair. `corner_ids`: the eight corners of a subdomain are the lattice vertices (c + a, s + b + 4 * e) for a, b, e in 0 and 1, taken modulo 2 and 16; each vertex has one number and is shared by eight subdomains. `dual_operator`: each subdomain's matrix is symmetric and positive definite. `dirichlet`: each subdomain's matrix is symmetric and positive definite. `coarse_inverse`: symmetric and positive definite.
All inputs are finite; a program needn't handle non-finite values.
Results may differ from a plain program's by a relative error of at most 0.0099.
Values sent between devices are 32-bit elements; how exact they have to be, the bound alone decides.
No kernel may reach another device: no remote copies, remote signals or barrier semaphores. Data moves between devices by JAX's collectives and lax.ppermute only.
A program may use at most 128 MiB of HBM per device.

v0:
```python
import jax
import jax.numpy as jnp
from jax import lax
from jax.sharding import PartitionSpec as P

ITERS = 2
STRIDE = 4


def padded(block, sides, width):
    for axis, dim in sides:
        count = lax.axis_size(axis)
        forward = [(i, i + 1) for i in range(count - 1)]
        forward.append((count - 1, 0))
        backward = [(target, source) for source, target in forward]
        low = lax.ppermute(
            lax.slice_in_dim(block, block.shape[dim] - width, None, axis=dim), axis, forward
        )
        high = lax.ppermute(lax.slice_in_dim(block, 0, width, axis=dim), axis, backward)
        block = jnp.concatenate([low, block, high], axis=dim)
    return block


def passed_along(value, axis, steps):
    count = lax.axis_size(axis)
    pairs = [(source, (source + steps) % count) for source in range(count)]
    return lax.ppermute(value, axis, pairs)


def local(
    load_terms,
    dual_operator,
    dirichlet,
    corner_coupling,
    coarse_inverse,
    face_map,
    face_live,
    corner_ids,
):
    local_loads = load_terms[0]
    operator_local = dual_operator[0]
    precond_local = dirichlet[0]
    coupling = corner_coupling[0]
    slot_maps = face_map[0]
    live_faces = face_live[0].astype(jnp.float32)
    corners = corner_ids[0]
    load_count = local_loads.shape[0]
    dual_size = local_loads.shape[1]
    face_size = dual_size // 6
    coarse_size = coarse_inverse.shape[1]
    coarse_index = (3 * corners[:, None] + jnp.arange(3, dtype=jnp.int32)[None, :]).reshape(-1)
    spread = (coarse_index[:, None] == jnp.arange(coarse_size, dtype=jnp.int32)[None, :]).astype(
        jnp.float32
    )

    def assemble(local_sum):
        face_parts = local_sum.reshape(load_count, 6, face_size)
        slab_pair = padded(jnp.stack([face_parts[:, 0], face_parts[:, 1]]), (("cluster", 0),), 1)
        row_pair = padded(jnp.stack([face_parts[:, 2], face_parts[:, 3]]), (("sub", 0),), 1)
        column_pair = []
        for source_face, shift_step in ((5, STRIDE), (4, -STRIDE)):
            column_pair.append(passed_along(face_parts[:, source_face], "sub", shift_step))
        received = [
            slab_pair[0],
            slab_pair[3],
            row_pair[0],
            row_pair[3],
            column_pair[0],
            column_pair[1],
        ]
        pieces = []
        for face_index in range(6):
            permuted = jnp.take(received[face_index], slot_maps[face_index], axis=1)
            pieces.append((face_parts[:, face_index] + permuted) * live_faces[face_index])
        return jnp.concatenate(pieces, axis=1)

    def precond_with_product(vector):
        local_term = jnp.dot(
            vector.astype(jnp.bfloat16), precond_local, preferred_element_type=jnp.float32
        )
        precond = assemble(local_term)
        product = 0.5 * lax.psum(jnp.sum(vector * precond, axis=1), ("cluster", "sub"))
        return (precond, product)

    right_side = assemble(local_loads)
    multipliers = jnp.zeros_like(right_side)
    residual = right_side
    precond, residual_dot = precond_with_product(residual)
    direction = precond
    for iteration in range(ITERS):
        rounded = direction.astype(jnp.bfloat16)
        direct = jnp.dot(rounded, operator_local, preferred_element_type=jnp.float32)
        corner_terms = jnp.dot(rounded, coupling, preferred_element_type=jnp.float32)
        coarse_local = jnp.dot(corner_terms, spread, precision=lax.Precision.HIGHEST)
        local_curve = jnp.sum(direction * direct, axis=1)
        apply_coarse_load, curve_total = lax.psum((coarse_local, local_curve), ("cluster", "sub"))
        own_values = jnp.dot(apply_coarse_load, coarse_inverse.T, precision=lax.Precision.HIGHEST)
        solution = lax.all_gather(own_values, ("cluster", "sub"), axis=1, tiled=True)
        corner_values = jnp.dot(solution, spread.T, precision=lax.Precision.HIGHEST).astype(
            jnp.bfloat16
        )
        back = lax.dot_general(
            corner_values, coupling, (((1,), (1,)), ((), ())), preferred_element_type=jnp.float32
        )
        dual_image = assemble(direct + back)
        curvature = curve_total + jnp.sum(apply_coarse_load * solution, axis=1)
        dual_image, curvature = (dual_image, curvature)
        step_size = residual_dot / curvature
        multipliers = multipliers + step_size[:, None] * direction
        residual = residual - step_size[:, None] * dual_image
        if iteration + 1 < ITERS:
            precond, residual_new = precond_with_product(residual)
            direction = precond + (residual_new / residual_dot)[:, None] * direction
            residual_dot = residual_new
    return (multipliers[None], residual[None])


def solution(mesh):
    placed = (
        P(("cluster", "sub"), None, None),
        P(("cluster", "sub"), None, None),
        P(("cluster", "sub"), None, None),
        P(("cluster", "sub"), None, None),
        P(("cluster", "sub"), None),
        P(("cluster", "sub"), None, None),
        P(("cluster", "sub"), None),
        P(("cluster", "sub"), None),
    )
    return jax.shard_map(
        local,
        mesh=mesh,
        in_specs=placed,
        out_specs=(P(("cluster", "sub"), None, None), P(("cluster", "sub"), None, None)),
        check_vma=False,
    )
```

profile of v0, /device:TPU:0, one launch (start us, length us, event | category | flops | bytes accessed | tf_op | source)
XLA Modules:
  0.0 432.1 jit_solution(1258101771140866283)
XLA Ops:
  2.3 3.0 collective-permute-start
  5.8 4.5 %collective-permute-start.3 = (f32[1,128,256]{2,1,0:T(8,128)S(1)}, f32[1,128,256]{2,1,0:T(8,128)S(1)}, u32[]{:S(2)}, u32[]{:S(2)}) collective-permute-start(f32[1,128,256]{2,1,0:T(8,128)S(1)} %bitcast.561), channel_id=1, source_target_pairs={{1,0},{2,1},{3,2},{4,3},{5,4},{6,5},{7,6},{8,7},{9,8},{10,9},{11,1... | collective-permute-start | bytes 393224 | tf_op jit(solution)/shard_map/ppermute | solution.py:19
  12.5 3.6 collective-permute-start.5
  16.1 6.6 %copy.173 = bf16[1,1536,1536]{1,2,0:T(8,128)(2,1)} copy(bf16[1,1536,1536]{2,1,0:T(8,128)(2,1)} %param.12) | data formatting | bytes 9437184 | tf_op args[2]
  33.2 4.0 fusion.6
  39.4 4.4 %collective-permute-start.9 = (f32[1,128,256]{2,1,0:T(8,128)S(1)}, f32[1,128,256]{2,1,0:T(8,128)S(1)}, u32[]{:S(2)}, u32[]{:S(2)}) collective-permute-start(f32[1,128,256]{2,1,0:T(8,128)S(1)} %get-tuple-element.30), channel_id=1, source_target_pairs={{1,0},{2,1},{3,2},{4,3},{5,4},{6,5},{7,6},{8,7},{9,8},{10,9},{11,1... | collective-permute-start | bytes 393224 | tf_op jit(solution)/shard_map/ppermute | solution.py:19
  44.0 3.9 collective-permute-start.11
  60.1 3.8 multiply_reduce_fusion.3
  65.1 37.5 %all-reduce.1 = (f32[128,96]{0,1:T(8,128)S(1)}, f32[128]{0:T(128)}, f32[128]{0:T(128)}) all-reduce(f32[128,96]{0,1:T(8,128)} %fusion.53, f32[128]{0:T(128)} %get-tuple-element.4, f32[128]{0:T(128)} %get-tuple-element.3), channel_id=1, replica_groups=mesh['cluster'=2,'sub'=16] {'cluster','sub'}, use_global_device_ids=true, to_apply=%region_4.6 | all-reduce | flops 12544 | bytes 100352 | tf_op jit(solution)/shard_map/psum | solution.py:96
  103.4 41.8 %all-gather = f32[32,3,128]{2,1,0:T(4,128)S(1)} all-gather(f32[1,3,128]{2,1,0:T(4,128)S(1)} %convolution_bitcast_fusion.1), channel_id=1, replica_groups=mesh['cluster'=2,'sub'=16] {'cluster','sub'}, dimensions={0}, use_global_device_ids=true | all-gather | bytes 50688 | tf_op jit(solution)/shard_map/all_gather | solution.py:98
  155.5 4.5 %collective-permute-start.15 = (f32[1,128,256]{2,1,0:T(8,128)S(1)}, f32[1,128,256]{2,1,0:T(8,128)}, u32[]{:S(2)}, u32[]{:S(2)}) collective-permute-start(f32[1,128,256]{2,1,0:T(8,128)S(1)} %bitcast.568), channel_id=1, source_target_pairs={{1,0},{2,1},{3,2},{4,3},{5,4},{6,5},{7,6},{8,7},{9,8},{10,9},{11,1... | collective-permute-start | bytes 393224 | tf_op jit(solution)/shard_map/ppermute | solution.py:19
  162.1 4.0 collective-permute-start.17
  200.6 4.3 fusion.4
  207.7 4.4 %collective-permute-start.21 = (f32[1,128,256]{2,1,0:T(8,128)}, f32[1,128,256]{2,1,0:T(8,128)}, u32[]{:S(2)}, u32[]{:S(2)}) collective-permute-start(f32[1,128,256]{2,1,0:T(8,128)} %get-tuple-element.18), channel_id=1, source_target_pairs={{1,0},{2,1},{3,2},{4,3},{5,4},{6,5},{7,6},{8,7},{9,8},{10,9},{11,1... | collective-permute-start | bytes 393224 | tf_op jit(solution)/shard_map/ppermute | solution.py:19
  212.2 3.8 collective-permute-start.23
  253.5 36.9 %psum.45 = f32[128]{0:T(128)S(1)} all-reduce(f32[128]{0:T(128)S(1)} %multiply_reduce_fusion.1), channel_id=1, replica_groups=mesh['cluster'=2,'sub'=16] {'cluster','sub'}, use_global_device_ids=true, to_apply=%region_7.9 | all-reduce | flops 128 | bytes 1024 | tf_op jit(solution)/shard_map/psum | solution.py:82
  292.4 4.3 multiply_reduce_fusion
  297.0 41.7 %all-reduce = (f32[128]{0:T(128)}, f32[128,96]{0,1:T(8,128)S(1)}) all-reduce(f32[128]{0:T(128)} %get-tuple-element.85, f32[128,96]{0,1:T(8,128)S(1)} %fusion.52), channel_id=1, replica_groups=mesh['cluster'=2,'sub'=16] {'cluster','sub'}, use_global_device_ids=true, to_apply=%region_9.11 | all-reduce | flops 12416 | bytes 99328 | tf_op jit(solution)/shard_map/psum | solution.py:96
  338.8 41.1 %all-gather.1 = f32[32,3,128]{2,1,0:T(4,128)S(1)} all-gather(f32[1,3,128]{2,1,0:T(4,128)S(1)} %convolution_bitcast_fusion), channel_id=1, replica_groups=mesh['cluster'=2,'sub'=16] {'cluster','sub'}, dimensions={0}, use_global_device_ids=true | all-gather | bytes 50688 | tf_op jit(solution)/shard_map/all_gather | solution.py:98
  388.5 4.5 %collective-permute-start.27 = (f32[1,128,256]{2,1,0:T(8,128)S(1)}, f32[1,128,256]{2,1,0:T(8,128)}, u32[]{:S(2)}, u32[]{:S(2)}) collective-permute-start(f32[1,128,256]{2,1,0:T(8,128)S(1)} %bitcast.573), channel_id=1, source_target_pairs={{1,0},{2,1},{3,2},{4,3},{5,4},{6,5},{7,6},{8,7},{9,8},{10,9},{11,1... | collective-permute-start | bytes 393224 | tf_op jit(solution)/shard_map/ppermute | solution.py:19
  395.5 3.8 collective-permute-start.29
  416.1 2.8 bitcast_dynamic-update-slice_fusion.10
  418.9 2.7 bitcast_dynamic-update-slice_fusion.9
  428.3 3.8 multiply_subtract_fusion
  (397 shorter events, 153.9 us)
Async XLA Ops:
  5.4 18.9 %collective-permute-start.1 = (f32[1,128,256]{2,1,0:T(8,128)S(1)}, f32[1,128,256]{2,1,0:T(8,128)S(1)}, u32[]{:S(2)}, u32[]{:S(2)}) collective-permute-start(f32[1,128,256]{2,1,0:T(8,128)S(1)} %bitcast.564), channel_id=1, source_target_pairs={{16,0},{0,16},{17,1},{1,17},{18,2},{2,18},{19,3},{3,19},{20,4},{4,... | collective-permute-start | bytes 393224 | tf_op jit(solution)/shard_map/ppermute | solution.py:19
  5.6 19.7 %collective-permute-start.2 = (f32[1,128,256]{2,1,0:T(8,128)S(1)}, f32[1,128,256]{2,1,0:T(8,128)S(1)}, u32[]{:S(2)}, u32[]{:S(2)}) collective-permute-start(f32[1,128,256]{2,1,0:T(8,128)S(1)} %bitcast.560), channel_id=1, source_target_pairs={{0,1},{1,2},{2,3},{3,4},{4,5},{5,6},{6,7},{7,8},{8,9},{9,10},{10,1... | collective-permute-start | bytes 393224 | tf_op jit(solution)/shard_map/ppermute | solution.py:16
  5.8 20.5 %collective-permute-start.3 = (f32[1,128,256]{2,1,0:T(8,128)S(1)}, f32[1,128,256]{2,1,0:T(8,128)S(1)}, u32[]{:S(2)}, u32[]{:S(2)}) collective-permute-start(f32[1,128,256]{2,1,0:T(8,128)S(1)} %bitcast.561), channel_id=1, source_target_pairs={{1,0},{2,1},{3,2},{4,3},{5,4},{6,5},{7,6},{8,7},{9,8},{10,9},{11,1... | collective-permute-start | bytes 393224 | tf_op jit(solution)/shard_map/ppermute | solution.py:19
  10.4 16.9 %collective-permute-start.4 = (f32[128,256]{1,0:T(8,128)S(1)}, f32[128,256]{1,0:T(8,128)S(1)}, u32[]{:S(2)}, u32[]{:S(2)}) collective-permute-start(f32[128,256]{1,0:T(8,128)S(1)} %bitcast.559), channel_id=1, source_target_pairs={{0,4},{1,5},{2,6},{3,7},{4,8},{5,9},{6,10},{7,11},{8,12},{9,13},{1... | collective-permute-start | bytes 393224 | tf_op jit(solution)/shard_map/ppermute | solution.py:27
  12.5 15.7 %collective-permute-start.5 = (f32[128,256]{1,0:T(8,128)S(1)}, f32[128,256]{1,0:T(8,128)S(1)}, u32[]{:S(2)}, u32[]{:S(2)}) collective-permute-start(f32[128,256]{1,0:T(8,128)S(1)} %bitcast.562), channel_id=1, source_target_pairs={{0,12},{1,13},{2,14},{3,15},{4,0},{5,1},{6,2},{7,3},{8,4},{9,5},{1... | collective-permute-start | bytes 393224 | tf_op jit(solution)/shard_map/ppermute | solution.py:27
  39.4 10.4 %collective-permute-start.8 = (f32[1,128,256]{2,1,0:T(8,128)S(1)}, f32[1,128,256]{2,1,0:T(8,128)S(1)}, u32[]{:S(2)}, u32[]{:S(2)}) collective-permute-start(f32[1,128,256]{2,1,0:T(8,128)S(1)} %get-tuple-element.32), channel_id=1, source_target_pairs={{0,1},{1,2},{2,3},{3,4},{4,5},{5,6},{6,7},{7,8},{8,9},{9,10},{10,1... | collective-permute-start | bytes 393224 | tf_op jit(solution)/shard_map/ppermute | solution.py:16
  39.4 11.3 %collective-permute-start.9 = (f32[1,128,256]{2,1,0:T(8,128)S(1)}, f32[1,128,256]{2,1,0:T(8,128)S(1)}, u32[]{:S(2)}, u32[]{:S(2)}) collective-permute-start(f32[1,128,256]{2,1,0:T(8,128)S(1)} %get-tuple-element.30), channel_id=1, source_target_pairs={{1,0},{2,1},{3,2},{4,3},{5,4},{6,5},{7,6},{8,7},{9,8},{10,9},{11,1... | collective-permute-start | bytes 393224 | tf_op jit(solution)/shard_map/ppermute | solution.py:19
  151.1 11.0 %collective-permute-start.12 = (f32[1,128,256]{2,1,0:T(8,128)S(1)}, f32[1,128,256]{2,1,0:T(8,128)S(1)}, u32[]{:S(2)}, u32[]{:S(2)}) collective-permute-start(f32[1,128,256]{2,1,0:T(8,128)S(1)} %bitcast.569), channel_id=1, source_target_pairs={{0,16},{16,0},{1,17},{17,1},{2,18},{18,2},{3,19},{19,3},{4,20},{20... | collective-permute-start | bytes 393224 | tf_op jit(solution)/shard_map/ppermute | solution.py:16
  152.3 17.9 %collective-permute-start.13 = (f32[1,128,256]{2,1,0:T(8,128)S(1)}, f32[1,128,256]{2,1,0:T(8,128)}, u32[]{:S(2)}, u32[]{:S(2)}) collective-permute-start(f32[1,128,256]{2,1,0:T(8,128)S(1)} %bitcast.570), channel_id=1, source_target_pairs={{16,0},{0,16},{17,1},{1,17},{18,2},{2,18},{19,3},{3,19},{20,4},{4,... | collective-permute-start | bytes 393224 | tf_op jit(solution)/shard_map/ppermute | solution.py:19
  155.3 18.9 %collective-permute-start.14 = (f32[1,128,256]{2,1,0:T(8,128)S(1)}, f32[1,128,256]{2,1,0:T(8,128)}, u32[]{:S(2)}, u32[]{:S(2)}) collective-permute-start(f32[1,128,256]{2,1,0:T(8,128)S(1)} %bitcast.567), channel_id=1, source_target_pairs={{0,1},{1,2},{2,3},{3,4},{4,5},{5,6},{6,7},{7,8},{8,9},{9,10},{10,1... | collective-permute-start | bytes 393224 | tf_op jit(solution)/shard_map/ppermute | solution.py:16
  155.5 22.7 %collective-permute-start.15 = (f32[1,128,256]{2,1,0:T(8,128)S(1)}, f32[1,128,256]{2,1,0:T(8,128)}, u32[]{:S(2)}, u32[]{:S(2)}) collective-permute-start(f32[1,128,256]{2,1,0:T(8,128)S(1)} %bitcast.568), channel_id=1, source_target_pairs={{1,0},{2,1},{3,2},{4,3},{5,4},{6,5},{7,6},{8,7},{9,8},{10,9},{11,1... | collective-permute-start | bytes 393224 | tf_op jit(solution)/shard_map/ppermute | solution.py:19
  161.0 21.3 %collective-permute-start.16 = (f32[128,256]{1,0:T(8,128)S(1)}, f32[128,256]{1,0:T(8,128)}, u32[]{:S(2)}, u32[]{:S(2)}) collective-permute-start(f32[128,256]{1,0:T(8,128)S(1)} %bitcast.565), channel_id=1, source_target_pairs={{0,4},{1,5},{2,6},{3,7},{4,8},{5,9},{6,10},{7,11},{8,12},{9,13},{1... | collective-permute-start | bytes 393224 | tf_op jit(solution)/shard_map/ppermute | solution.py:27
  162.1 25.8 %collective-permute-start.17 = (f32[128,256]{1,0:T(8,128)S(1)}, f32[128,256]{1,0:T(8,128)}, u32[]{:S(2)}, u32[]{:S(2)}) collective-permute-start(f32[128,256]{1,0:T(8,128)S(1)} %bitcast.566), channel_id=1, source_target_pairs={{0,12},{1,13},{2,14},{3,15},{4,0},{5,1},{6,2},{7,3},{8,4},{9,5},{1... | collective-permute-start | bytes 393224 | tf_op jit(solution)/shard_map/ppermute | solution.py:27
  205.8 14.2 %collective-permute-start.19 = (f32[1,128,256]{2,1,0:T(8,128)}, f32[1,128,256]{2,1,0:T(8,128)}, u32[]{:S(2)}, u32[]{:S(2)}) collective-permute-start(f32[1,128,256]{2,1,0:T(8,128)} %get-tuple-element.17), channel_id=1, source_target_pairs={{16,0},{0,16},{17,1},{1,17},{18,2},{2,18},{19,3},{3,19},{20,4},{4,... | collective-permute-start | bytes 393224 | tf_op jit(solution)/shard_map/ppermute | solution.py:19
  207.7 16.3 %collective-permute-start.20 = (f32[1,128,256]{2,1,0:T(8,128)}, f32[1,128,256]{2,1,0:T(8,128)}, u32[]{:S(2)}, u32[]{:S(2)}) collective-permute-start(f32[1,128,256]{2,1,0:T(8,128)} %get-tuple-element.20), channel_id=1, source_target_pairs={{0,1},{1,2},{2,3},{3,4},{4,5},{5,6},{6,7},{7,8},{8,9},{9,10},{10,1... | collective-permute-start | bytes 393224 | tf_op jit(solution)/shard_map/ppermute | solution.py:16
  207.7 20.3 %collective-permute-start.21 = (f32[1,128,256]{2,1,0:T(8,128)}, f32[1,128,256]{2,1,0:T(8,128)}, u32[]{:S(2)}, u32[]{:S(2)}) collective-permute-start(f32[1,128,256]{2,1,0:T(8,128)} %get-tuple-element.18), channel_id=1, source_target_pairs={{1,0},{2,1},{3,2},{4,3},{5,4},{6,5},{7,6},{8,7},{9,8},{10,9},{11,1... | collective-permute-start | bytes 393224 | tf_op jit(solution)/shard_map/ppermute | solution.py:19
  212.2 19.9 %collective-permute-start.22 = (f32[128,256]{1,0:T(8,128)}, f32[128,256]{1,0:T(8,128)}, u32[]{:S(2)}, u32[]{:S(2)}) collective-permute-start(f32[128,256]{1,0:T(8,128)} %get-tuple-element.19), channel_id=1, source_target_pairs={{0,4},{1,5},{2,6},{3,7},{4,8},{5,9},{6,10},{7,11},{8,12},{9,13},{1... | collective-permute-start | bytes 393224 | tf_op jit(solution)/shard_map/ppermute | solution.py:27
  212.2 26.1 %collective-permute-start.23 = (f32[128,256]{1,0:T(8,128)}, f32[128,256]{1,0:T(8,128)}, u32[]{:S(2)}, u32[]{:S(2)}) collective-permute-start(f32[128,256]{1,0:T(8,128)} %get-tuple-element.16), channel_id=1, source_target_pairs={{0,12},{1,13},{2,14},{3,15},{4,0},{5,1},{6,2},{7,3},{8,4},{9,5},{1... | collective-permute-start | bytes 393224 | tf_op jit(solution)/shard_map/ppermute | solution.py:27
  383.2 12.3 %collective-permute-start.24 = (f32[1,128,256]{2,1,0:T(8,128)S(1)}, f32[1,128,256]{2,1,0:T(8,128)S(1)}, u32[]{:S(2)}, u32[]{:S(2)}) collective-permute-start(f32[1,128,256]{2,1,0:T(8,128)S(1)} %bitcast.574), channel_id=1, source_target_pairs={{0,16},{16,0},{1,17},{17,1},{2,18},{18,2},{3,19},{19,3},{4,20},{20... | collective-permute-start | bytes 393224 | tf_op jit(solution)/shard_map/ppermute | solution.py:16
  384.5 17.3 %collective-permute-start.25 = (f32[1,128,256]{2,1,0:T(8,128)S(1)}, f32[1,128,256]{2,1,0:T(8,128)}, u32[]{:S(2)}, u32[]{:S(2)}) collective-permute-start(f32[1,128,256]{2,1,0:T(8,128)S(1)} %bitcast.575), channel_id=1, source_target_pairs={{16,0},{0,16},{17,1},{1,17},{18,2},{2,18},{19,3},{3,19},{20,4},{4,... | collective-permute-start | bytes 393224 | tf_op jit(solution)/shard_map/ppermute | solution.py:19
  387.4 17.0 %collective-permute-start.26 = (f32[1,128,256]{2,1,0:T(8,128)S(1)}, f32[1,128,256]{2,1,0:T(8,128)}, u32[]{:S(2)}, u32[]{:S(2)}) collective-permute-start(f32[1,128,256]{2,1,0:T(8,128)S(1)} %bitcast.572), channel_id=1, source_target_pairs={{0,1},{1,2},{2,3},{3,4},{4,5},{5,6},{6,7},{7,8},{8,9},{9,10},{10,1... | collective-permute-start | bytes 393224 | tf_op jit(solution)/shard_map/ppermute | solution.py:16
  388.5 18.4 %collective-permute-start.27 = (f32[1,128,256]{2,1,0:T(8,128)S(1)}, f32[1,128,256]{2,1,0:T(8,128)}, u32[]{:S(2)}, u32[]{:S(2)}) collective-permute-start(f32[1,128,256]{2,1,0:T(8,128)S(1)} %bitcast.573), channel_id=1, source_target_pairs={{1,0},{2,1},{3,2},{4,3},{5,4},{6,5},{7,6},{8,7},{9,8},{10,9},{11,1... | collective-permute-start | bytes 393224 | tf_op jit(solution)/shard_map/ppermute | solution.py:19
  394.0 15.5 %collective-permute-start.28 = (f32[128,256]{1,0:T(8,128)S(1)}, f32[128,256]{1,0:T(8,128)}, u32[]{:S(2)}, u32[]{:S(2)}) collective-permute-start(f32[128,256]{1,0:T(8,128)S(1)} %bitcast.571), channel_id=1, source_target_pairs={{0,4},{1,5},{2,6},{3,7},{4,8},{5,9},{6,10},{7,11},{8,12},{9,13},{1... | collective-permute-start | bytes 393224 | tf_op jit(solution)/shard_map/ppermute | solution.py:27
  395.5 16.5 %collective-permute-start.29 = (f32[128,256]{1,0:T(8,128)}, f32[128,256]{1,0:T(8,128)}, u32[]{:S(2)}, u32[]{:S(2)}) collective-permute-start(f32[128,256]{1,0:T(8,128)} %bitcast.155), channel_id=1, source_target_pairs={{0,12},{1,13},{2,14},{3,15},{4,0},{5,1},{6,2},{7,3},{8,4},{9,5},{1... | collective-permute-start | bytes 393224 | tf_op jit(solution)/shard_map/ppermute | solution.py:27
  (87 other events, 1831.2 us)
where the time goes:
time: 434 us; the launch traced here: 432 us
  blocking collectives  199 us (46%)
  local copies, waits for them, and re-layouts  101 us (23%)
  starting transfers between devices  53.7 us (12%)
  other arithmetic  53 us (12%)
  matrix products  23.2 us (5%)
    all_gather x2, blocking collectives, local(): lax.all_gather(own_values, ('cluster', 'sub'), axis=1, tiled=True)  82.9 us
    psum x2, blocking collectives, local(): lax.psum((coarse_local, local_curve), ('cluster', 'sub'))  79.2 us
    gather x60, local copies, waits for them, and re-layouts, assemble(): permuted = jnp.take(received[face_index], slot_maps[face_index], axis=1)  55.5 us
    unnamed x25, other arithmetic  39.7 us
    psum x1, blocking collectives, precond_with_product(): lax.psum(jnp.sum(vector * precond, axis=1), ('cluster', 'sub'))  36.9 us
    ppermute x10, starting transfers between devices, padded(): lax.ppermute(lax.slice_in_dim(block, 0, width, axis=dim), axis, backward)  28.2 us
    unnamed x184, local copies, waits for them, and re-layouts  20.4 us
    ppermute x10, starting transfers between devices, passed_along(): return lax.ppermute(value, axis, pairs)  19.6 us
  transfers between devices with their start and end apart: 30, of which 0 were waited for; matrix products, arithmetic and copies ran while one was open for 20% of the time, Pallas kernels for 0%

commit v1 on v0

v1 whole, which is shorter than its diff:
```python
import functools

import jax
import jax.numpy as jnp
from jax import lax
from jax.experimental import pallas as pl
from jax.experimental.pallas import tpu as pltpu
from jax.sharding import PartitionSpec as P

ITERS = 2
STRIDE = 4
LANES = 128
AXES = ("cluster", "sub")
EXACT = lax.Precision.HIGHEST
F32 = jnp.float32
BF16 = jnp.bfloat16
VMEM = pl.BlockSpec(memory_space=pltpu.VMEM)
SMEM = pl.BlockSpec(memory_space=pltpu.SMEM)
ANY = pl.BlockSpec(memory_space=pl.ANY)


def shifted(value, axis, steps):
    count = lax.axis_size(axis)
    return lax.ppermute(value, axis, [(i, (i + steps) % count) for i in range(count)])


def exchange(faces):
    return (
        shifted(faces[1], "cluster", 1),
        shifted(faces[0], "cluster", -1),
        shifted(faces[3], "sub", 1),
        shifted(faces[2], "sub", -1),
        shifted(faces[5], "sub", STRIDE),
        shifted(faces[4], "sub", -STRIDE),
    )


def spread_out(chunks):
    return lax.all_to_all(chunks, AXES, 0, 0, tiled=True)


def call(body, outs, ins, operands, scratch=(), flops=0, moved=0):
    return pl.pallas_call(
        body,
        out_shape=tuple(jax.ShapeDtypeStruct(shape, dtype) for shape, dtype in outs),
        in_specs=list(ins),
        out_specs=tuple(VMEM for _ in outs),
        scratch_shapes=list(scratch),
        compiler_params=pltpu.CompilerParams(vmem_limit_bytes=40 << 20),
        cost_estimate=pl.CostEstimate(flops=flops, bytes_accessed=moved, transcendentals=0),
    )(*operands)


def mapped(part, slots):
    rows = part.shape[0]
    tiles = part.shape[1] // LANES
    pieces = []
    for tile in range(tiles):
        index = jnp.broadcast_to(slots[:, tile * LANES : (tile + 1) * LANES], (rows, LANES))
        inside = index & (LANES - 1)
        out = None
        for source in range(tiles):
            found = jnp.take_along_axis(
                part[:, source * LANES : (source + 1) * LANES],
                inside,
                axis=1,
                mode="promise_in_bounds",
            )
            out = found if out is None else jnp.where(index >= source * LANES, found, out)
        pieces.append(out)
    return jnp.concatenate(pieces, axis=1)


def as_columns(row, width):
    count = row.shape[1]
    tall = jnp.broadcast_to(row, (count, count)).T
    return jnp.concatenate([tall] * (width // count), axis=1)


def row_sums(value):
    total = jnp.sum(value, axis=1, keepdims=True)
    return jnp.broadcast_to(total, (value.shape[0], value.shape[0])).T[0:1]


def column_ids(ids):
    rows = []
    for corner in range(ids.shape[0]):
        for part in range(3):
            rows.append(ids[corner : corner + 1] * 3.0 + float(part))
    return jnp.concatenate(rows, axis=0)


def local(
    load_terms,
    dual_operator,
    dirichlet,
    corner_coupling,
    coarse_inverse,
    face_map,
    face_live,
    corner_ids,
):
    count, size = load_terms.shape[1:]
    face = face_map.shape[2]
    terms = corner_coupling.shape[2]
    corners = corner_ids.shape[1]
    own, coarse = coarse_inverse.shape
    devices = lax.axis_size("cluster") * lax.axis_size("sub")
    tiles = -(-coarse // LANES)
    wide = tiles * LANES
    sent = 8 * (-(-(own + 2) // 8))
    gathered = 8 * (-(-(own * (1 + tiles)) // 8))
    coupling = corner_coupling[0].T
    operator = dual_operator[0]
    precond = dirichlet[0]
    loads = load_terms[0]
    slots = face_map[0]
    field = (count, size)
    part = (count, face)
    longer = count + terms + corners
    matmul_flops = 2 * count * size * size

    def cut(index):
        return slice(index * face, (index + 1) * face)

    def fetch(matrix, held, sems):
        copies = []
        for index in range(6):
            copy = pltpu.make_async_copy(
                matrix.at[pl.ds(index * face, face)],
                held.at[pl.ds(index * face, face)],
                sems.at[index],
            )
            copy.start()
            copies.append(copy)
        return copies

    matrix_scratch = [pltpu.VMEM((size, size), BF16), pltpu.SemaphoreType.DMA((6,))]

    def first_faces(loads_ref, coupling_ref, ids_ref, *outs):
        for index in range(6):
            outs[index][0:count] = loads_ref[:, cut(index)]
            outs[index][count : count + terms] = coupling_ref[:, cut(index)].astype(F32)
            for corner in range(corners):
                outs[index][count + terms + corner : count + terms + corner + 1] = jnp.full(
                    (1, face), ids_ref[0, corner].astype(F32)
                )

    def start(loads_ref, *refs):
        received = refs[0:6]
        slots_ref, live_ref, matrix, residual_ref = refs[6:10]
        faces = refs[10:16]
        dot_ref, held, sems = refs[16:19]
        copies = fetch(matrix, held, sems)
        total = None
        for index in range(6):
            live = live_ref[0, index].astype(F32)
            value = loads_ref[:, cut(index)] + mapped(
                received[index][0:count], slots_ref[index : index + 1]
            )
            value = value * live
            residual_ref[:, cut(index)] = value
            copies[index].wait()
            product = jnp.dot(value.astype(BF16), held[cut(index)], preferred_element_type=F32)
            total = product if total is None else total + product
        for index in range(6):
            faces[index][...] = total[:, cut(index)]
        dot_ref[...] = jnp.broadcast_to(row_sums(total * residual_ref[...]), dot_ref.shape)

    def to_targets(ids_ref, coupling_ref, rounded, rows, chunks_ref):
        corner_rows = lax.dot_general(
            coupling_ref[...], rounded, (((1,), (1,)), ((), ())), preferred_element_type=F32
        )
        extra = jnp.concatenate(rows + [jnp.zeros_like(rows[0])] * (8 - len(rows)), axis=0)
        stacked = jnp.concatenate([corner_rows, extra], axis=0)
        shape = (devices * sent, terms + 8)
        line = lax.broadcasted_iota(jnp.int32, shape, 0)
        lane = lax.broadcasted_iota(jnp.int32, (1, terms + 8), 1)
        target = jnp.full((1, terms + 8), -1, jnp.int32)
        for corner in range(corners):
            for component in range(3):
                number = ids_ref[0, corner] * 3 + component
                place = (number // own) * sent + number % own
                target = jnp.where(lane == corner * 3 + component, place, target)
        chosen = line == target
        within = line % sent
        column = lax.broadcasted_iota(jnp.int32, shape, 1)
        for at in range(len(rows)):
            chosen = chosen | ((column == terms + at) & (within == own + at))
        block = jnp.dot(
            chosen.astype(F32), stacked, precision=EXACT, preferred_element_type=F32
        )
        chunks_ref[...] = block.reshape(devices, sent, count)

    def apply_operator(direction_faces, copies, held):
        total = None
        for index in range(6):
            copies[index].wait()
            product = jnp.dot(direction_faces[index], held[cut(index)], preferred_element_type=F32)
            total = product if total is None else total + product
        return total

    def first_image(*refs):
        own_faces, received = refs[0:6], refs[6:12]
        slots_ref, live_ref, matrix, coupling_ref, ids_ref, dot_ref = refs[12:18]
        direction_ref = refs[18]
        faces = refs[19:25]
        chunks_ref, held, sems = refs[25:28]
        copies = fetch(matrix, held, sems)
        rounded = []
        for index in range(6):
            live = live_ref[0, index].astype(F32)
            value = own_faces[index][...] + mapped(
                received[index][...], slots_ref[index : index + 1]
            )
            value = value * live
            direction_ref[:, cut(index)] = value
            rounded.append(value.astype(BF16))
        total = apply_operator(rounded, copies, held)
        for index in range(6):
            faces[index][...] = total[:, cut(index)]
        curve = row_sums(total * direction_ref[...])
        to_targets(
            ids_ref, coupling_ref, jnp.concatenate(rounded, axis=1), [dot_ref[0:1], curve], chunks_ref
        )

    def next_image(*refs):
        own_faces, received = refs[0:6], refs[6:12]
        slots_ref, live_ref, matrix, coupling_ref, ids_ref = refs[12:17]
        before_ref, dots_ref, totals_ref = refs[17:20]
        direction_ref = refs[20]
        faces = refs[21:27]
        chunks_ref, new_ref, held, sems = refs[27:31]
        copies = fetch(matrix, held, sems)
        new_dot = jnp.sum(dots_ref[...], axis=0)[0:1]
        new_ref[...] = jnp.broadcast_to(new_dot, new_ref.shape)
        ratio = as_columns(new_dot / totals_ref[own : own + 1], face)
        rounded = []
        for index in range(6):
            live = live_ref[0, index].astype(F32)
            value = own_faces[index][...] + mapped(
                received[index][...], slots_ref[index : index + 1]
            )
            value = value * live + ratio * before_ref[:, cut(index)]
            direction_ref[:, cut(index)] = value
            rounded.append(value.astype(BF16))
        total = apply_operator(rounded, copies, held)
        for index in range(6):
            faces[index][...] = total[:, cut(index)]
        curve = row_sums(total * direction_ref[...])
        to_targets(
            ids_ref, coupling_ref, jnp.concatenate(rounded, axis=1), [curve, curve], chunks_ref
        )

    def relay(with_inverse, chunks_ref, *refs):
        totals = jnp.sum(chunks_ref[...], axis=0)
        if with_inverse:
            inverse_ref, out_ref, totals_ref = refs
            rows = [totals[0:own]]
            for tile in range(tiles):
                piece = inverse_ref[:, tile * LANES : min((tile + 1) * LANES, coarse)]
                if piece.shape[1] < LANES:
                    piece = jnp.concatenate(
                        [piece, jnp.zeros((own, LANES - piece.shape[1]), F32)], axis=1
                    )
                rows.append(piece)
            rest = gathered - own * (1 + tiles)
            if rest:
                rows.append(jnp.zeros((rest, LANES), F32))
            out_ref[...] = jnp.broadcast_to(jnp.concatenate(rows, axis=0)[None], out_ref.shape)
        else:
            out_ref, totals_ref = refs
            out_ref[...] = jnp.broadcast_to(totals[None], out_ref.shape)
        totals_ref[...] = totals

    def corner_values(load, inverse, numbers):
        solved = jnp.dot(inverse, load, precision=EXACT, preferred_element_type=F32)
        energy = jnp.sum(solved * load[0:coarse], axis=0, keepdims=True)
        lane = lax.broadcasted_iota(jnp.int32, (terms, coarse), 1).astype(F32)
        values = []
        for number in numbers:
            chosen = (lane == number).astype(F32)
            values.append(
                jnp.dot(chosen, solved, precision=EXACT, preferred_element_type=F32).astype(BF16)
            )
        return values, energy

    def coarse_part(value, coupling_rows):
        return lax.dot_general(
            value, coupling_rows, (((0,), (0,)), ((), ())), preferred_element_type=F32
        )

    def numbers_of(ids, width):
        return column_ids(jnp.broadcast_to(ids[:, 0:1], (corners, width)))

    def gather_load(gathered_ref, load_ref):
        for device in range(devices):
            load_ref[device * own : (device + 1) * own] = gathered_ref[device, 0:own]
        if wide > coarse:
            load_ref[coarse:wide] = jnp.zeros((wide - coarse, count), F32)

    def image_face(index, faces, received, own_first, other_first, slots_ref, live_ref, values):
        live = live_ref[0, index].astype(F32)
        slots_row = slots_ref[index : index + 1]
        other = mapped(other_first[index][count : count + terms], slots_row).astype(BF16)
        value = faces[index][...] + mapped(received[index][...], slots_row)
        value = value + coarse_part(values[0], own_first[:, cut(index)])
        value = value + coarse_part(values[1 + index], other)
        return value * live

    def all_values(load_ref, inverse, ids_ref, other_first):
        corner_rows = [jnp.full((1, coarse), ids_ref[0, c].astype(F32)) for c in range(corners)]
        numbers = [column_ids(jnp.concatenate(corner_rows, axis=0))]
        for index in range(6):
            numbers.append(numbers_of(other_first[index][count + terms : longer], coarse))
        return corner_values(load_ref[...], inverse, numbers)

    def second_residual(*refs):
        faces, received, other_first = refs[0:6], refs[6:12], refs[12:18]
        slots_ref, live_ref, matrix, coupling_ref, ids_ref = refs[18:23]
        before_ref, gathered_ref, totals_ref = refs[23:26]
        residual_ref = refs[26]
        outs = refs[27:33]
        chunks_ref, inverse_ref, step_ref, load_ref, held, sems = refs[33:39]
        copies = fetch(matrix, held, sems)
        gather_load(gathered_ref, load_ref)
        for device in range(devices):
            for tile in range(tiles):
                inverse_ref[
                    device * own : (device + 1) * own, tile * LANES : (tile + 1) * LANES
                ] = gathered_ref[device, own * (1 + tile) : own * (2 + tile)]
        values, energy = all_values(load_ref, inverse_ref[...], ids_ref, other_first)
        step = totals_ref[own : own + 1] / (totals_ref[own + 1 : own + 2] + energy)
        step_ref[...] = jnp.broadcast_to(step, step_ref.shape)
        scale = as_columns(step, face)
        total = None
        for index in range(6):
            image = image_face(
                index, faces, received, coupling_ref, other_first, slots_ref, live_ref, values
            )
            value = before_ref[:, cut(index)] - scale * image
            residual_ref[:, cut(index)] = value
            copies[index].wait()
            product = jnp.dot(value.astype(BF16), held[cut(index)], preferred_element_type=F32)
            total = product if total is None else total + product
        for index in range(6):
            outs[index][...] = total[:, cut(index)]
        chunks_ref[...] = jnp.broadcast_to(
            row_sums(total * residual_ref[...])[None], chunks_ref.shape
        )

    def finish(*refs):
        faces, received, other_first = refs[0:6], refs[6:12], refs[12:18]
        slots_ref, live_ref, coupling_ref, ids_ref = refs[18:22]
        before_ref, gathered_ref, totals_ref, inverse_ref = refs[22:26]
        first_ref, second_ref, step_ref, fresh_ref = refs[26:30]
        multipliers_ref, residual_ref, load_ref = refs[30:33]
        gather_load(gathered_ref, load_ref)
        values, energy = all_values(load_ref, inverse_ref[...], ids_ref, other_first)
        step = fresh_ref[0:1] / (totals_ref[own + 1 : own + 2] + energy)
        scale = as_columns(step, face)
        earlier = as_columns(step_ref[0:1], face)
        for index in range(6):
            image = image_face(
                index, faces, received, coupling_ref, other_first, slots_ref, live_ref, values
            )
            residual_ref[:, cut(index)] = before_ref[:, cut(index)] - scale * image
            multipliers_ref[:, cut(index)] = (
                earlier * first_ref[:, cut(index)] + scale * second_ref[:, cut(index)]
            )

    six = [(part, F32)] * 6
    row = ((8, count), F32)
    sent_block = ((devices, sent, count), F32)
    fixed = [VMEM, SMEM]

    opening = call(
        first_faces, [((longer, face), F32)] * 6, [VMEM, VMEM, SMEM], (loads, coupling, corner_ids)
    )
    other_first = exchange(opening)
    residual, *faces, dot = call(
        start,
        [(field, F32)] + six + [row],
        [VMEM] * 7 + fixed + [ANY],
        (loads, *other_first, slots, face_live, precond),
        matrix_scratch,
        flops=matmul_flops,
    )
    received = exchange(faces)
    direction, *images, chunks = call(
        first_image,
        [(field, F32)] + six + [sent_block],
        [VMEM] * 12 + fixed + [ANY, VMEM, SMEM, VMEM],
        (*faces, *received, slots, face_live, operator, coupling, corner_ids, dot),
        matrix_scratch,
        flops=matmul_flops,
    )
    arrived = exchange(images)
    block, totals = call(
        functools.partial(relay, True),
        [((devices, gathered, count), F32), ((sent, count), F32)],
        [VMEM, VMEM],
        (spread_out(chunks), coarse_inverse),
    )
    second, *faces, dots, inverse, step = call(
        second_residual,
        [(field, F32)] + six + [((devices, 1, count), F32), ((coarse, wide), F32), row],
        [VMEM] * 18 + fixed + [ANY, VMEM, SMEM, VMEM, VMEM, VMEM],
        (
            *images,
            *arrived,
            *other_first,
            slots,
            face_live,
            precond,
            coupling,
            corner_ids,
            residual,
            spread_out(block),
            totals,
        ),
        [pltpu.VMEM((wide, count), F32)] + matrix_scratch,
        flops=matmul_flops,
    )
    received = exchange(faces)
    following, *images, chunks, fresh = call(
        next_image,
        [(field, F32)] + six + [sent_block, row],
        [VMEM] * 12 + fixed + [ANY, VMEM, SMEM, VMEM, VMEM, VMEM],
        (
            *faces,
            *received,
            slots,
            face_live,
            operator,
            coupling,
            corner_ids,
            direction,
            spread_out(dots),
            totals,
        ),
        matrix_scratch,
        flops=matmul_flops,
    )
    arrived = exchange(images)
    block, totals = call(
        functools.partial(relay, False),
        [sent_block, ((sent, count), F32)],
        [VMEM],
        (spread_out(chunks),),
    )
    multipliers, last = call(
        finish,
        [(field, F32)] * 2,
        [VMEM] * 18 + fixed + [VMEM, SMEM] + [VMEM] * 8,
        (
            *images,
            *arrived,
            *other_first,
            slots,
            face_live,
            coupling,
            corner_ids,
            second,
            spread_out(block),
            totals,
            inverse,
            direction,
            following,
            step,
            fresh,
        ),
        [pltpu.VMEM((wide, count), F32)],
    )
    return (multipliers[None], last[None])


def solution(mesh):
    placed = (
        P(AXES, None, None),
        P(AXES, None, None),
        P(AXES, None, None),
        P(AXES, None, None),
        P(AXES, None),
        P(AXES, None, None),
        P(AXES, None),
        P(AXES, None),
    )
    return jax.shard_map(
        local,
        mesh=mesh,
        in_specs=placed,
        out_specs=(P(AXES, None, None), P(AXES, None, None)),
        check_vma=False,
    )
```

time: 434 us -> 170 us (0.39)
  blocking collectives: 199 us -> 11.1 us
  other arithmetic: 53 us -> 0.01 us
  local copies, waits for them, and re-layouts: 101 us -> 51.7 us
  waiting for transfers between devices: 0.08 us -> 34 us
  matrix products: 23.2 us -> 0 us
  Pallas kernels: 0 us -> 16.3 us
    psum x3 -> x0, blocking collectives: 116 us -> none  [the longest x2 79.2 us: local(): lax.psum((coarse_local, local_curve), ('cluster', 'sub'))]
    all_gather x2 -> x0, blocking collectives: 82.9 us -> none  [local(): lax.all_gather(own_values, ('cluster', 'sub'), axis=1, tiled=True)]
    gather x60 -> x0, local copies, waits for them, and re-layouts: 55.5 us -> none  [assemble(): permuted = jnp.take(received[face_index], slot_maps[face_index], axis=1)]
    unnamed x25 -> x1, other arithmetic: 39.7 us -> 0.01 us
    unnamed x184 -> x145, local copies, waits for them, and re-layouts: 20.4 us -> 51.7 us
    dot_general x14 -> x0, matrix products: 23.2 us -> none  [the longest x2 8.22 us: precond_with_product(): jnp.dot(vector.astype(jnp.bfloat16), precond_local, preferred_element_typ...]
    ppermute x30, waiting for transfers between devices: 0.08 us -> 21.1 us  [shifted(): lax.ppermute(value, axis, [(i, (i + steps) % count) for i in range(count)])]
    pallas_call x0 -> x8, Pallas kernels: none -> 16.3 us  [call(): pl.pallas_call(body, out_shape=tuple((jax.ShapeDtypeStruct(shape, dtype)...]
  transfers between devices with their start and end apart: 30 -> 34, of which waited for: 0 -> 16; matrix products, arithmetic and copies ran while one was open for 20% -> 0% of each run, Pallas kernels for 0% -> 0%
where the time goes in v1:
time: 170 us; the launch traced here: 169 us
  starting transfers between devices  54.6 us (32%)
  local copies, waits for them, and re-layouts  51.7 us (30%)
  waiting for transfers between devices  34 us (20%)
  Pallas kernels  16.3 us (10%)
  blocking collectives  11.1 us (7%)
    unnamed x145, local copies, waits for them, and re-layouts  51.7 us
    ppermute x30, starting transfers between devices, shifted(): lax.ppermute(value, axis, [(i, (i + steps) % count) for i in range(count)])  42.8 us
    ppermute x30, waiting for transfers between devices, shifted(): lax.ppermute(value, axis, [(i, (i + steps) % count) for i in range(count)])  21.1 us
    pallas_call x8, Pallas kernels, call(): pl.pallas_call(body, out_shape=tuple((jax.ShapeDtypeStruct(shape, dtype)...  16.3 us
    all_to_all x4, waiting for transfers between devices, spread_out(): return lax.all_to_all(chunks, AXES, 0, 0, tiled=True)  12.9 us
    all_to_all x4, starting transfers between devices, spread_out(): return lax.all_to_all(chunks, AXES, 0, 0, tiled=True)  11.7 us
    all_to_all x1, blocking collectives, spread_out(): return lax.all_to_all(chunks, AXES, 0, 0, tiled=True)  11.1 us
  transfers between devices with their start and end apart: 34, of which 16 were waited for; matrix products, arithmetic and copies ran while one was open for 0% of the time, Pallas kernels for 0%

profile of v1, /device:TPU:0, one launch (start us, length us, event | category | flops | bytes accessed | tf_op | source)
XLA Modules:
  0.0 168.6 jit_solution(9678007968185104326)
XLA Ops:
  3.9 3.0 %collective-permute-start = (f32[160,256]{1,0:T(8,128)S(1)}, f32[160,256]{1,0:T(8,128)S(1)}, u32[]{:S(2)}, u32[]{:S(2)}) collective-permute-start(f32[160,256]{1,0:T(8,128)S(1)} %get-tuple-element.49), channel_id=1, source_target_pairs={{0,16},{16,0},{1,17},{17,1},{2,18},{18,2},{3,19},{19,3},{4,20},{20... | collective-permute-start | bytes 491528 | tf_op jit(solution)/shard_map/ppermute | solution.py:24
  7.0 4.4 %collective-permute-start.3 = (f32[160,256]{1,0:T(8,128)S(1)}, f32[160,256]{1,0:T(8,128)S(1)}, u32[]{:S(2)}, u32[]{:S(2)}) collective-permute-start(f32[160,256]{1,0:T(8,128)S(1)} %get-tuple-element.52), channel_id=1, source_target_pairs={{0,15},{1,0},{2,1},{3,2},{4,3},{5,4},{6,5},{7,6},{8,7},{9,8},{10,9... | collective-permute-start | bytes 491528 | tf_op jit(solution)/shard_map/ppermute | solution.py:24
  12.0 4.1 %collective-permute-start.5 = (f32[160,256]{1,0:T(8,128)S(1)}, f32[160,256]{1,0:T(8,128)S(1)}, u32[]{:S(2)}, u32[]{:S(2)}) collective-permute-start(f32[160,256]{1,0:T(8,128)S(1)} %get-tuple-element.54), channel_id=1, source_target_pairs={{0,12},{1,13},{2,14},{3,15},{4,0},{5,1},{6,2},{7,3},{8,4},{9,5},{1... | collective-permute-start | bytes 491528 | tf_op jit(solution)/shard_map/ppermute | solution.py:24
  16.8 3.9 %collective-permute-done.4.refs_4_.refs_16_ = f32[160,256]{1,0:T(8,128)S(1)} collective-permute-done((f32[160,256]{1,0:T(8,128)S(1)}, f32[160,256]{1,0:T(8,128)S(1)}, u32[]{:S(2)}, u32[]{:S(2)}) %collective-permute-start.4) | collective-permute-done | bytes 163872 | tf_op jit(solution)/shard_map/ppermute | solution.py:24
  21.8 2.3 %copy-done = bf16[1,1536,1536]{2,1,0:T(8,128)(2,1)S(1)} copy-done((bf16[1,1536,1536]{2,1,0:T(8,128)(2,1)S(1)}, bf16[1,1536,1536]{2,1,0:T(8,128)(2,1)}, u32[]{:S(2)}) %copy-start) | copy-done | bytes 4718616
  24.8 2.4 %shard_map.96 = (f32[128,1536]{1,0:T(8,128)S(1)}, f32[128,256]{1,0:T(8,128)S(1)}, f32[128,256]{1,0:T(8,128)S(1)}, f32[128,256]{1,0:T(8,128)S(1)}, f32[128,256]{1...) custom-call(f32[128,1536]{1,0:T(8,128)S(1)} %bitcast.18, ...), custom_call_target="tpu_custom_call" | custom-call | flops 603979776 | tf_op jit(solution)/shard_map/pallas_call | solution.py:43
  34.6 2.9 %collective-permute-done.8.refs_8_ = f32[128,256]{1,0:T(8,128)S(1)} collective-permute-done((f32[128,256]{1,0:T(8,128)S(1)}, f32[128,256]{1,0:T(8,128)S(1)}, u32[]{:S(2)}, u32[]{:S(2)}) %collective-permute-start.8) | collective-permute-done | bytes 131104 | tf_op jit(solution)/shard_map/ppermute | solution.py:24
  37.5 3.5 %collective-permute-done.10.refs_10_ = f32[128,256]{1,0:T(8,128)S(1)} collective-permute-done((f32[128,256]{1,0:T(8,128)S(1)}, f32[128,256]{1,0:T(8,128)S(1)}, u32[]{:S(2)}, u32[]{:S(2)}) %collective-permute-start.10) | collective-permute-done | bytes 131104 | tf_op jit(solution)/shard_map/ppermute | solution.py:24
  41.0 3.1 %shard_map.97 = (f32[128,1536]{1,0:T(8,128)S(1)}, f32[128,256]{1,0:T(8,128)S(1)}, f32[128,256]{1,0:T(8,128)S(1)}, f32[128,256]{1,0:T(8,128)S(1)}, f32[128,256]{1...) custom-call(f32[128,256]{1,0:T(8,128)S(1)} %get-tuple-element.55.refs_0_, ...), custom_call_target="tpu_custom_call" | custom-call | flops 603979776 | tf_op jit(solution)/shard_map/pallas_call | solution.py:43
  44.8 4.0 %all-to-all-start = ((f32[32,8,128]{2,1,0:T(8,128)}), f32[32,8,128]{2,1,0:T(8,128)S(1)}, u32[]{:S(2)}, u32[]{:S(2)}) async-start(f32[32,8,128]{2,1,0:T(8,128)} %copy-done.52), calls=%async_computation | async-start | bytes 262144 | tf_op jit(solution)/shard_map/all_to_all | solution.py:39
  50.6 6.4 %all-to-all-done.chunks_ref = f32[32,8,128]{2,1,0:T(8,128)S(1)} async-done(((f32[32,8,128]{2,1,0:T(8,128)}), f32[32,8,128]{2,1,0:T(8,128)S(1)}, u32[]{:S(2)}, u32[]{:S(2)}) %all-to-all-start) | async-done | bytes 131104 | tf_op jit(solution)/shard_map/all_to_all | solution.py:39
  59.0 2.6 %all-to-all-start.1 = ((f32[32,8,128]{2,1,0:T(8,128)}), f32[32,8,128]{2,1,0:T(8,128)S(1)}, u32[]{:S(2)}, u32[]{:S(2)}) async-start(f32[32,8,128]{2,1,0:T(8,128)} %copy-done.50), calls=%async_computation.1 | async-start | bytes 262144 | tf_op jit(solution)/shard_map/all_to_all | solution.py:39
  63.2 3.8 %collective-permute-start.15 = (f32[128,256]{1,0:T(8,128)S(1)}, f32[128,256]{1,0:T(8,128)S(1)}, u32[]{:S(2)}, u32[]{:S(2)}) collective-permute-start(f32[128,256]{1,0:T(8,128)S(1)} %get-tuple-element.64.refs_2_), channel_id=1, source_target_pairs={{0,15},{1,0},{2,1},{3,2},{4,3},{5,4},{6,5},{7,6},{8,7},{9,8},{10,9... | collective-permute-start | bytes 393224 | tf_op jit(solution)/shard_map/ppermute | solution.py:24
  71.4 2.8 %collective-permute-done.14.refs_8_ = f32[128,256]{1,0:T(8,128)S(1)} collective-permute-done((f32[128,256]{1,0:T(8,128)S(1)}, f32[128,256]{1,0:T(8,128)S(1)}, u32[]{:S(2)}, u32[]{:S(2)}) %collective-permute-start.14) | collective-permute-done | bytes 131104 | tf_op jit(solution)/shard_map/ppermute | solution.py:24
  76.8 2.3 %copy-done.1 = bf16[1,1536,1536]{2,1,0:T(8,128)(2,1)S(1)} copy-done((bf16[1,1536,1536]{2,1,0:T(8,128)(2,1)S(1)}, bf16[1,1536,1536]{2,1,0:T(8,128)(2,1)}, u32[]{:S(2)}) %copy-start.1) | copy-done | bytes 4718616
  91.3 3.9 %shard_map.99 = (f32[128,1536]{1,0:T(8,128)S(1)}, f32[128,256]{1,0:T(8,128)S(1)}, f32[128,256]{1,0:T(8,128)S(1)}, f32[128,256]{1,0:T(8,128)S(1)}, f32[128,256]{1...) custom-call(f32[128,256]{1,0:T(8,128)S(1)} %get-tuple-element.62.ref, ...), custom_call_target="tpu_custom_call" | custom-call | flops 603979776 | tf_op jit(solution)/shard_map/pallas_call | solution.py:43
  102.6 11.1 %all_to_all.25.refs_18_ = f32[32,1,128]{2,1,0:T(1,128)S(1)} all-to-all(f32[32,1,128]{2,1,0:T(1,128)S(1)} %get-tuple-element.79), channel_id=1, replica_groups=mesh['cluster'=2,'sub'=16] {'cluster','sub'}, dimensions={0} | all-to-all | bytes 32768 | tf_op jit(solution)/shard_map/all_to_all | solution.py:39
  113.8 3.1 %shard_map.100 = (f32[128,1536]{1,0:T(8,128)S(1)}, f32[128,256]{1,0:T(8,128)S(1)}, f32[128,256]{1,0:T(8,128)S(1)}, f32[128,256]{1,0:T(8,128)S(1)}, f32[128,256]{...) custom-call(f32[128,256]{1,0:T(8,128)S(1)} %get-tuple-element.72.ref, ...), custom_call_target="tpu_custom_call" | custom-call | flops 603979776 | tf_op jit(solution)/shard_map/pallas_call | solution.py:43
  121.7 2.6 %all-to-all-start.3 = ((f32[32,8,128]{2,1,0:T(8,128)}), f32[32,8,128]{2,1,0:T(8,128)S(1)}, u32[]{:S(2)}, u32[]{:S(2)}) async-start(f32[32,8,128]{2,1,0:T(8,128)} %copy-done.51), calls=%async_computation.3 | async-start | bytes 262144 | tf_op jit(solution)/shard_map/all_to_all | solution.py:39
  125.9 6.5 %all-to-all-done.3.chunks_ref = f32[32,8,128]{2,1,0:T(8,128)S(1)} async-done(((f32[32,8,128]{2,1,0:T(8,128)}), f32[32,8,128]{2,1,0:T(8,128)S(1)}, u32[]{:S(2)}, u32[]{:S(2)}) %all-to-all-start.3) | async-done | bytes 131104 | tf_op jit(solution)/shard_map/all_to_all | solution.py:39
  133.7 2.6 %all-to-all-start.4 = ((f32[32,8,128]{2,1,0:T(8,128)}), f32[32,8,128]{2,1,0:T(8,128)S(1)}, u32[]{:S(2)}, u32[]{:S(2)}) async-start(f32[32,8,128]{2,1,0:T(8,128)} %get-tuple-element.88), calls=%async_computation.4 | async-start | bytes 262144 | tf_op jit(solution)/shard_map/all_to_all | solution.py:39
  138.0 3.8 %collective-permute-start.27 = (f32[128,256]{1,0:T(8,128)}, f32[128,256]{1,0:T(8,128)S(1)}, u32[]{:S(2)}, u32[]{:S(2)}) collective-permute-start(f32[128,256]{1,0:T(8,128)} %copy-done.30), channel_id=1, source_target_pairs={{0,15},{1,0},{2,1},{3,2},{4,3},{5,4},{6,5},{7,6},{8,7},{9,8},{10,9... | collective-permute-start | bytes 393224 | tf_op jit(solution)/shard_map/ppermute | solution.py:24
  146.5 2.7 %collective-permute-done.26.refs_8_ = f32[128,256]{1,0:T(8,128)S(1)} collective-permute-done((f32[128,256]{1,0:T(8,128)}, f32[128,256]{1,0:T(8,128)S(1)}, u32[]{:S(2)}, u32[]{:S(2)}) %collective-permute-start.26) | collective-permute-done | bytes 131104 | tf_op jit(solution)/shard_map/ppermute | solution.py:24
  166.1 2.5 %shard_map.102 = (f32[128,1536]{1,0:T(8,128)}, f32[128,1536]{1,0:T(8,128)}) custom-call(f32[128,256]{1,0:T(8,128)S(1)} %get-tuple-element.80.refs_0_, f32[128,256]{1,0:T(8,128)S(1)} %get-tuple-element.81.refs_1_, f32[128,256]{1,0:T(8,128)S(1)} %copy-done.31, f32[128,256]{1,0:T(8,128)S(1)} %copy-done.33, f32[128,256]{1,0:T(8,128)S(1)} %copy-done.35, ...), custom_call_target="tpu_custom_call" | custom-call | tf_op jit(solution)/shard_map/pallas_call | solution.py:43
  (199 shorter events, 77.3 us)
Async XLA Ops:
  3.9 8.1 %collective-permute-start = (f32[160,256]{1,0:T(8,128)S(1)}, f32[160,256]{1,0:T(8,128)S(1)}, u32[]{:S(2)}, u32[]{:S(2)}) collective-permute-start(f32[160,256]{1,0:T(8,128)S(1)} %get-tuple-element.49), channel_id=1, source_target_pairs={{0,16},{16,0},{1,17},{17,1},{2,18},{18,2},{3,19},{19,3},{4,20},{20... | collective-permute-start | bytes 491528 | tf_op jit(solution)/shard_map/ppermute | solution.py:24
  7.0 9.9 %collective-permute-start.1 = (f32[160,256]{1,0:T(8,128)S(1)}, f32[160,256]{1,0:T(8,128)S(1)}, u32[]{:S(2)}, u32[]{:S(2)}) collective-permute-start(f32[160,256]{1,0:T(8,128)S(1)} %get-tuple-element.50), channel_id=1, source_target_pairs={{0,16},{16,0},{1,17},{17,1},{2,18},{18,2},{3,19},{19,3},{4,20},{20... | collective-permute-start | bytes 491528 | tf_op jit(solution)/shard_map/ppermute | solution.py:24
  7.0 9.8 %collective-permute-start.2 = (f32[160,256]{1,0:T(8,128)S(1)}, f32[160,256]{1,0:T(8,128)S(1)}, u32[]{:S(2)}, u32[]{:S(2)}) collective-permute-start(f32[160,256]{1,0:T(8,128)S(1)} %get-tuple-element.51), channel_id=1, source_target_pairs={{0,1},{1,2},{2,3},{3,4},{4,5},{5,6},{6,7},{7,8},{8,9},{9,10},{10,1... | collective-permute-start | bytes 491528 | tf_op jit(solution)/shard_map/ppermute | solution.py:24
  7.0 9.8 %collective-permute-start.3 = (f32[160,256]{1,0:T(8,128)S(1)}, f32[160,256]{1,0:T(8,128)S(1)}, u32[]{:S(2)}, u32[]{:S(2)}) collective-permute-start(f32[160,256]{1,0:T(8,128)S(1)} %get-tuple-element.52), channel_id=1, source_target_pairs={{0,15},{1,0},{2,1},{3,2},{4,3},{5,4},{6,5},{7,6},{8,7},{9,8},{10,9... | collective-permute-start | bytes 491528 | tf_op jit(solution)/shard_map/ppermute | solution.py:24
  11.5 9.2 %collective-permute-start.4 = (f32[160,256]{1,0:T(8,128)S(1)}, f32[160,256]{1,0:T(8,128)S(1)}, u32[]{:S(2)}, u32[]{:S(2)}) collective-permute-start(f32[160,256]{1,0:T(8,128)S(1)} %get-tuple-element.53), channel_id=1, source_target_pairs={{0,4},{1,5},{2,6},{3,7},{4,8},{5,9},{6,10},{7,11},{8,12},{9,13},{1... | collective-permute-start | bytes 491528 | tf_op jit(solution)/shard_map/ppermute | solution.py:24
  12.0 9.8 %collective-permute-start.5 = (f32[160,256]{1,0:T(8,128)S(1)}, f32[160,256]{1,0:T(8,128)S(1)}, u32[]{:S(2)}, u32[]{:S(2)}) collective-permute-start(f32[160,256]{1,0:T(8,128)S(1)} %get-tuple-element.54), channel_id=1, source_target_pairs={{0,12},{1,13},{2,14},{3,15},{4,0},{5,1},{6,2},{7,3},{8,4},{9,5},{1... | collective-permute-start | bytes 491528 | tf_op jit(solution)/shard_map/ppermute | solution.py:24
  33.1 7.9 %collective-permute-start.10 = (f32[128,256]{1,0:T(8,128)S(1)}, f32[128,256]{1,0:T(8,128)S(1)}, u32[]{:S(2)}, u32[]{:S(2)}) collective-permute-start(f32[128,256]{1,0:T(8,128)S(1)} %get-tuple-element.60.refs_5_), channel_id=1, source_target_pairs={{0,4},{1,5},{2,6},{3,7},{4,8},{5,9},{6,10},{7,11},{8,12},{9,13},{1... | collective-permute-start | bytes 393224 | tf_op jit(solution)/shard_map/ppermute | solution.py:24
  44.8 12.3 %all-to-all-start = ((f32[32,8,128]{2,1,0:T(8,128)}), f32[32,8,128]{2,1,0:T(8,128)S(1)}, u32[]{:S(2)}, u32[]{:S(2)}) async-start(f32[32,8,128]{2,1,0:T(8,128)} %copy-done.52), calls=%async_computation | async-start | bytes 262144 | tf_op jit(solution)/shard_map/all_to_all | solution.py:39
  48.8 18.8 %collective-permute-start.13 = (f32[128,256]{1,0:T(8,128)S(1)}, f32[128,256]{1,0:T(8,128)S(1)}, u32[]{:S(2)}, u32[]{:S(2)}) collective-permute-start(f32[128,256]{1,0:T(8,128)S(1)} %get-tuple-element.62.refs_0_), channel_id=1, source_target_pairs={{0,16},{16,0},{1,17},{17,1},{2,18},{18,2},{3,19},{19,3},{4,20},{20... | collective-permute-start | bytes 393224 | tf_op jit(solution)/shard_map/ppermute | solution.py:24
  59.0 17.8 %all-to-all-start.1 = ((f32[32,8,128]{2,1,0:T(8,128)}), f32[32,8,128]{2,1,0:T(8,128)S(1)}, u32[]{:S(2)}, u32[]{:S(2)}) async-start(f32[32,8,128]{2,1,0:T(8,128)} %copy-done.50), calls=%async_computation.1 | async-start | bytes 262144 | tf_op jit(solution)/shard_map/all_to_all | solution.py:39
  61.5 8.2 %collective-permute-start.12 = (f32[128,256]{1,0:T(8,128)S(1)}, f32[128,256]{1,0:T(8,128)S(1)}, u32[]{:S(2)}, u32[]{:S(2)}) collective-permute-start(f32[128,256]{1,0:T(8,128)S(1)} %get-tuple-element.63.refs_1_), channel_id=1, source_target_pairs={{0,16},{16,0},{1,17},{17,1},{2,18},{18,2},{3,19},{19,3},{4,20},{20... | collective-permute-start | bytes 393224 | tf_op jit(solution)/shard_map/ppermute | solution.py:24
  68.2 7.9 %collective-permute-start.16 = (f32[128,256]{1,0:T(8,128)S(1)}, f32[128,256]{1,0:T(8,128)S(1)}, u32[]{:S(2)}, u32[]{:S(2)}) collective-permute-start(f32[128,256]{1,0:T(8,128)S(1)} %get-tuple-element.67.refs_5_), channel_id=1, source_target_pairs={{0,4},{1,5},{2,6},{3,7},{4,8},{5,9},{6,10},{7,11},{8,12},{9,13},{1... | collective-permute-start | bytes 393224 | tf_op jit(solution)/shard_map/ppermute | solution.py:24
  96.0 17.7 %collective-permute-start.18 = (f32[128,256]{1,0:T(8,128)S(1)}, f32[128,256]{1,0:T(8,128)S(1)}, u32[]{:S(2)}, u32[]{:S(2)}) collective-permute-start(f32[128,256]{1,0:T(8,128)S(1)} %get-tuple-element.73.refs_1_), channel_id=1, source_target_pairs={{0,16},{16,0},{1,17},{17,1},{2,18},{18,2},{3,19},{19,3},{4,20},{20... | collective-permute-start | bytes 393224 | tf_op jit(solution)/shard_map/ppermute | solution.py:24
  97.3 16.4 %collective-permute-start.21 = (f32[128,256]{1,0:T(8,128)S(1)}, f32[128,256]{1,0:T(8,128)S(1)}, u32[]{:S(2)}, u32[]{:S(2)}) collective-permute-start(f32[128,256]{1,0:T(8,128)S(1)} %get-tuple-element.74.refs_2_), channel_id=1, source_target_pairs={{0,15},{1,0},{2,1},{3,2},{4,3},{5,4},{6,5},{7,6},{8,7},{9,8},{10,9... | collective-permute-start | bytes 393224 | tf_op jit(solution)/shard_map/ppermute | solution.py:24
  98.7 15.1 %collective-permute-start.20 = (f32[128,256]{1,0:T(8,128)S(1)}, f32[128,256]{1,0:T(8,128)S(1)}, u32[]{:S(2)}, u32[]{:S(2)}) collective-permute-start(f32[128,256]{1,0:T(8,128)S(1)} %get-tuple-element.75.refs_3_), channel_id=1, source_target_pairs={{0,1},{1,2},{2,3},{3,4},{4,5},{5,6},{6,7},{7,8},{8,9},{9,10},{10,1... | collective-permute-start | bytes 393224 | tf_op jit(solution)/shard_map/ppermute | solution.py:24
  98.7 15.1 %collective-permute-start.23 = (f32[128,256]{1,0:T(8,128)S(1)}, f32[128,256]{1,0:T(8,128)S(1)}, u32[]{:S(2)}, u32[]{:S(2)}) collective-permute-start(f32[128,256]{1,0:T(8,128)S(1)} %get-tuple-element.76.refs_4_), channel_id=1, source_target_pairs={{0,12},{1,13},{2,14},{3,15},{4,0},{5,1},{6,2},{7,3},{8,4},{9,5},{1... | collective-permute-start | bytes 393224 | tf_op jit(solution)/shard_map/ppermute | solution.py:24
  101.7 12.1 %collective-permute-start.22 = (f32[128,256]{1,0:T(8,128)S(1)}, f32[128,256]{1,0:T(8,128)S(1)}, u32[]{:S(2)}, u32[]{:S(2)}) collective-permute-start(f32[128,256]{1,0:T(8,128)S(1)} %get-tuple-element.77.refs_5_), channel_id=1, source_target_pairs={{0,4},{1,5},{2,6},{3,7},{4,8},{5,9},{6,10},{7,11},{8,12},{9,13},{1... | collective-permute-start | bytes 393224 | tf_op jit(solution)/shard_map/ppermute | solution.py:24
  121.7 10.8 %all-to-all-start.3 = ((f32[32,8,128]{2,1,0:T(8,128)}), f32[32,8,128]{2,1,0:T(8,128)S(1)}, u32[]{:S(2)}, u32[]{:S(2)}) async-start(f32[32,8,128]{2,1,0:T(8,128)} %copy-done.51), calls=%async_computation.3 | async-start | bytes 262144 | tf_op jit(solution)/shard_map/all_to_all | solution.py:39
  124.2 18.1 %collective-permute-start.25 = (f32[128,256]{1,0:T(8,128)S(1)}, f32[128,256]{1,0:T(8,128)S(1)}, u32[]{:S(2)}, u32[]{:S(2)}) collective-permute-start(f32[128,256]{1,0:T(8,128)S(1)} %get-tuple-element.80.refs_0_), channel_id=1, source_target_pairs={{0,16},{16,0},{1,17},{17,1},{2,18},{18,2},{3,19},{19,3},{4,20},{20... | collective-permute-start | bytes 393224 | tf_op jit(solution)/shard_map/ppermute | solution.py:24
  133.7 18.0 %all-to-all-start.4 = ((f32[32,8,128]{2,1,0:T(8,128)}), f32[32,8,128]{2,1,0:T(8,128)S(1)}, u32[]{:S(2)}, u32[]{:S(2)}) async-start(f32[32,8,128]{2,1,0:T(8,128)} %get-tuple-element.88), calls=%async_computation.4 | async-start | bytes 262144 | tf_op jit(solution)/shard_map/all_to_all | solution.py:39
  136.3 8.2 %collective-permute-start.24 = (f32[128,256]{1,0:T(8,128)S(1)}, f32[128,256]{1,0:T(8,128)S(1)}, u32[]{:S(2)}, u32[]{:S(2)}) collective-permute-start(f32[128,256]{1,0:T(8,128)S(1)} %get-tuple-element.81.refs_1_), channel_id=1, source_target_pairs={{0,16},{16,0},{1,17},{17,1},{2,18},{18,2},{3,19},{19,3},{4,20},{20... | collective-permute-start | bytes 393224 | tf_op jit(solution)/shard_map/ppermute | solution.py:24
  138.0 7.8 %collective-permute-start.27 = (f32[128,256]{1,0:T(8,128)}, f32[128,256]{1,0:T(8,128)S(1)}, u32[]{:S(2)}, u32[]{:S(2)}) collective-permute-start(f32[128,256]{1,0:T(8,128)} %copy-done.30), channel_id=1, source_target_pairs={{0,15},{1,0},{2,1},{3,2},{4,3},{5,4},{6,5},{7,6},{8,7},{9,8},{10,9... | collective-permute-start | bytes 393224 | tf_op jit(solution)/shard_map/ppermute | solution.py:24
  141.8 7.9 %collective-permute-start.29 = (f32[128,256]{1,0:T(8,128)}, f32[128,256]{1,0:T(8,128)S(1)}, u32[]{:S(2)}, u32[]{:S(2)}) collective-permute-start(f32[128,256]{1,0:T(8,128)} %copy-done.34), channel_id=1, source_target_pairs={{0,12},{1,13},{2,14},{3,15},{4,0},{5,1},{6,2},{7,3},{8,4},{9,5},{1... | collective-permute-start | bytes 393224 | tf_op jit(solution)/shard_map/ppermute | solution.py:24
  143.0 8.1 %collective-permute-start.28 = (f32[128,256]{1,0:T(8,128)}, f32[128,256]{1,0:T(8,128)S(1)}, u32[]{:S(2)}, u32[]{:S(2)}) collective-permute-start(f32[128,256]{1,0:T(8,128)} %copy-done.36), channel_id=1, source_target_pairs={{0,4},{1,5},{2,6},{3,7},{4,8},{5,9},{6,10},{7,11},{8,12},{9,13},{1... | collective-permute-start | bytes 393224 | tf_op jit(solution)/shard_map/ppermute | solution.py:24
  (82 other events, 436.5 us)

commit v2 on v0

v2 whole, which is shorter than its diff:
```python
import jax
import jax.numpy as jnp
from jax import lax
from jax.experimental import pallas as pl
from jax.experimental.pallas import tpu as pltpu
from jax.sharding import PartitionSpec as P

STRIDE = 4
LANES = 128
AXES = ("cluster", "sub")
EXACT = lax.Precision.HIGHEST
F32 = jnp.float32
BF16 = jnp.bfloat16
HBM = pl.BlockSpec(memory_space=pltpu.HBM)
NT = (((1,), (1,)), ((), ()))
TN = (((0,), (0,)), ((), ()))


def shifted(value, axis, steps):
    count = lax.axis_size(axis)
    return lax.ppermute(value, axis, [(i, (i + steps) % count) for i in range(count)])


def exchange(faces):
    return [
        shifted(faces[1], "cluster", 1),
        shifted(faces[0], "cluster", -1),
        shifted(faces[3], "sub", 1),
        shifted(faces[2], "sub", -1),
        shifted(faces[5], "sub", STRIDE),
        shifted(faces[4], "sub", -STRIDE),
    ]


def spread_out(chunks):
    return lax.all_to_all(chunks, AXES, 0, 0, tiled=True)


class Loaded:
    def __init__(self, source, held, sems, parts):
        rows = source.shape[0] // parts
        self.held = held
        self.copies = []
        for part in range(parts):
            where = pl.ds(part * rows, rows)
            self.copies.append(
                pltpu.make_async_copy(source.at[where], held.at[where], sems.at[part])
            )
            self.copies[part].start()
        self.waited = [False] * parts

    def ref(self, part=0):
        if not self.waited[part]:
            self.copies[part].wait()
            self.waited[part] = True
        return self.held


def run(body, ins, outs, flops=0, parts=None):
    parts = parts or {}
    names = list(ins)
    results = list(outs)
    pieces = [parts.get(name, 1) for name in names]

    def kernel(*refs):
        sources = refs[: len(names)]
        targets = refs[len(names) : len(names) + len(results)]
        rest = refs[len(names) + len(results) :]
        held = rest[: len(names)]
        made = rest[len(names) : len(names) + len(results)]
        sems = rest[len(names) + len(results) : 2 * len(names) + len(results)]
        out_sems = rest[-1]
        loaded = {}
        for at, name in enumerate(names):
            loaded[name] = Loaded(sources[at], held[at], sems[at], pieces[at])
        buffers = dict(zip(results, made, strict=True))
        started = []

        def send(name):
            at = results.index(name)
            copy = pltpu.make_async_copy(made[at], targets[at], out_sems.at[at])
            copy.start()
            started.append(copy)

        body(lambda name, part=0: loaded[name].ref(part), buffers, send)
        for name in names:
            for part in range(parts.get(name, 1)):
                loaded[name].ref(part)
        for copy in started:
            copy.wait()

    moved = sum(v.size * v.dtype.itemsize for v in ins.values())
    out = pl.pallas_call(
        kernel,
        out_shape=tuple(jax.ShapeDtypeStruct(*outs[name]) for name in results),
        in_specs=[HBM] * len(names),
        out_specs=tuple(HBM for _ in results),
        scratch_shapes=[pltpu.VMEM(ins[name].shape, ins[name].dtype) for name in names]
        + [pltpu.VMEM(*outs[name]) for name in results]
        + [pltpu.SemaphoreType.DMA((count,)) for count in pieces]
        + [pltpu.SemaphoreType.DMA((len(results),))],
        compiler_params=pltpu.CompilerParams(vmem_limit_bytes=67043328),
        cost_estimate=pl.CostEstimate(flops=flops, bytes_accessed=moved, transcendentals=0),
    )(*ins.values())
    return dict(zip(results, out, strict=True))


def mapped(part, slots):
    rows = part.shape[0]
    tiles = part.shape[1] // LANES
    pieces = []
    for tile in range(tiles):
        index = jnp.broadcast_to(slots[:, tile * LANES : (tile + 1) * LANES], (rows, LANES))
        inside = index & (LANES - 1)
        out = None
        for source in range(tiles):
            found = jnp.take_along_axis(
                part[:, source * LANES : (source + 1) * LANES],
                inside,
                axis=1,
                mode="promise_in_bounds",
            )
            out = found if out is None else jnp.where(index >= source * LANES, found, out)
        pieces.append(out)
    return jnp.concatenate(pieces, axis=1)


def as_columns(row, width):
    count = row.shape[1]
    tall = jnp.broadcast_to(row, (count, count)).T
    return jnp.concatenate([tall] * (width // count), axis=1)


def row_sums(value):
    total = jnp.sum(value, axis=1, keepdims=True)
    return jnp.broadcast_to(total, (value.shape[0], value.shape[0])).T[0:1]


def local(
    load_terms,
    dual_operator,
    dirichlet,
    corner_coupling,
    coarse_inverse,
    face_map,
    face_live,
    corner_ids,
):
    count, size = load_terms.shape[1:]
    face = face_map.shape[2]
    terms = corner_coupling.shape[2]
    corners = corner_ids.shape[1]
    own, coarse = coarse_inverse.shape
    devices = lax.axis_size("cluster") * lax.axis_size("sub")
    assert own == 3
    tiles = -(-coarse // LANES)
    wide = tiles * LANES
    sent = 8
    at_curve = own * (1 + tiles)
    gathered = 8 * (-(-(at_curve + 2) // 8))
    named = 7 * terms
    coupling = corner_coupling[0].T
    field = ((count, size), F32)
    part = ((count, face), F32)
    longer = count + terms + corners
    matmul_flops = 2 * count * size * size
    six = {"face%d" % index: part for index in range(6)}
    rows8 = ((8, count), F32)
    sent_block = ((devices, sent, count), F32)

    def cut(index):
        return slice(index * face, (index + 1) * face)

    def opening(loads_ref, coupling_ref, live_ref, ids_ref, *outs):
        for index in range(6):
            outs[index][0:count] = loads_ref[:, cut(index)]
            outs[index][count : count + terms] = coupling_ref[:, cut(index)].astype(F32)
            for corner in range(corners):
                outs[index][count + terms + corner : count + terms + corner + 1] = jnp.full(
                    (1, face), ids_ref[0, corner].astype(F32)
                )
        info = outs[6]
        for index in range(6):
            info[index : index + 1] = jnp.full((1, face), live_ref[0, index].astype(F32))
        info[6:8] = jnp.zeros((2, face), F32)
        for corner in range(corners):
            info[8 + corner : 9 + corner] = jnp.full((1, face), ids_ref[0, corner].astype(F32))

    def numbers_of(ids):
        made = []
        for corner in range(corners):
            for component in range(3):
                made.append(ids[corner : corner + 1] * 3.0 + float(component))
        return jnp.concatenate(made, axis=0)

    def assembled(get, index, own_part, received):
        slots = get("slots")[index : index + 1]
        return (own_part + mapped(received, slots)) * get("info")[index : index + 1]

    def times_matrix(get, total, index, value):
        product = jnp.dot(
            value.astype(BF16), get("matrix", index)[cut(index)], preferred_element_type=F32
        )
        return product if total is None else total + product

    def scatter_loads(get, image, couplings, numbers, dot):
        first = None
        others = []
        for index in range(6):
            value = image[:, cut(index)] * get("info")[index : index + 1]
            high = value.astype(BF16)
            low = (value - high.astype(F32)).astype(BF16)
            both = lax.dot_general(
                couplings(index),
                jnp.concatenate([high, low], axis=0),
                NT,
                preferred_element_type=F32,
            )
            both = both[:, 0:count] + both[:, count : 2 * count]
            first = both[0:terms] if first is None else first + both[0:terms]
            others.append(both[terms : 2 * terms])
        stacked = jnp.concatenate(
            [first] + others + [dot, jnp.zeros((7, count), F32)], axis=0
        )
        vertex = jnp.floor((numbers + 0.5) * (1.0 / 3.0))
        place = (numbers + vertex * float(sent - 3)).astype(jnp.int32)
        shape = (named + 8, devices * sent)
        place = jnp.concatenate([place] * (shape[1] // LANES), axis=1)
        lane = lax.broadcasted_iota(jnp.int32, shape, 1)
        line = lax.broadcasted_iota(jnp.int32, shape, 0)
        chosen = (line < named) & (lane == place)
        chosen = chosen | ((line == named) & ((lane & (sent - 1)) == own))
        block = lax.dot_general(
            chosen.astype(F32), stacked, TN, precision=EXACT, preferred_element_type=F32
        )
        return block.reshape(devices, sent, count)

    def gather_chunk(get, totals, extra):
        made = [totals[0:own]]
        for tile in range(tiles):
            piece = get("inverse")[:, tile * LANES : min((tile + 1) * LANES, coarse)]
            if piece.shape[1] < LANES:
                piece = jnp.concatenate(
                    [piece, jnp.zeros((own, LANES - piece.shape[1]), F32)], axis=1
                )
            made.append(piece)
        made.extend(extra)
        rest = gathered - at_curve - len(extra)
        if rest:
            made.append(jnp.zeros((rest, LANES), F32))
        return jnp.broadcast_to(
            jnp.concatenate(made, axis=0)[None], (devices, gathered, count)
        )

    def solve_coarse(get):
        block = get("block")
        load = [block[device, 0:own] for device in range(devices)]
        if wide > coarse:
            load.append(jnp.zeros((wide - coarse, count), F32))
        load = jnp.concatenate(load, axis=0)
        solved = None
        for tile in range(tiles):
            begin = own * (1 + tile)
            inverse = jnp.concatenate(
                [block[device, begin : begin + own] for device in range(devices)], axis=0
            )
            product = jnp.dot(
                inverse,
                load[tile * LANES : (tile + 1) * LANES],
                precision=EXACT,
                preferred_element_type=F32,
            )
            solved = product if solved is None else solved + product
        energy = jnp.sum(solved * load[0:coarse], axis=0, keepdims=True)
        lane = lax.broadcasted_iota(jnp.int32, (named, wide), 1)
        numbers = jnp.concatenate([get("numbers")[0:named]] * tiles, axis=1)
        chosen = (lane == numbers.astype(jnp.int32)).astype(F32)
        if wide > coarse:
            solved = jnp.concatenate([solved, jnp.zeros((wide - coarse, count), F32)], axis=0)
        values = jnp.dot(chosen, solved, precision=EXACT, preferred_element_type=F32)
        sums = jnp.sum(block[:, at_curve : at_curve + 2], axis=0)
        return values.astype(BF16), energy, sums

    def image_face(get, index, values):
        begin = terms * (1 + index)
        corner = jnp.concatenate([values[0:terms], values[begin : begin + terms]], axis=0)
        rows = jnp.concatenate(
            [get("coupling")[:, cut(index)], get("other")[:, cut(index)]], axis=0
        )
        back = lax.dot_general(corner, rows, TN, preferred_element_type=F32)
        return assembled(
            get, index, get("face%d" % index)[...] + back, get("received%d" % index)[...]
        )

    def start(get, out, send):
        total = None
        ids = [jnp.broadcast_to(get("info")[8:16][:, 0:1], (corners, LANES))]
        for index in range(6):
            received = get("received%d" % index)
            value = assembled(get, index, get("loads")[:, cut(index)], received[0:count])
            out["residual"][:, cut(index)] = value
            total = times_matrix(get, total, index, value)
        send("residual")
        for index in range(6):
            out["face%d" % index][...] = total[:, cut(index)]
            send("face%d" % index)
        for index in range(6):
            received = get("received%d" % index)
            rows = mapped(received[count : count + terms], get("slots")[index : index + 1])
            out["other"][:, cut(index)] = rows.astype(BF16)
            ids.append(
                jnp.broadcast_to(received[count + terms : longer][:, 0:1], (corners, LANES))
            )
        send("other")
        numbers = jnp.concatenate(
            [numbers_of(value) for value in ids] + [jnp.full((8, LANES), -1.0, F32)], axis=0
        )
        out["numbers"][...] = numbers
        send("numbers")
        out["chunks"][...] = scatter_loads(
            get,
            total,
            lambda index: jnp.concatenate(
                [get("coupling")[:, cut(index)], out["other"][:, cut(index)]], axis=0
            ),
            numbers,
            row_sums(total * out["residual"][...]),
        )
        send("chunks")

    def image(get, out, send, later):
        total = None
        for index in range(6):
            value = assembled(
                get, index, get("face%d" % index)[...], get("received%d" % index)[...]
            )
            out["direction"][:, cut(index)] = value
            total = times_matrix(get, total, index, value)
        send("direction")
        for index in range(6):
            out["face%d" % index][...] = total[:, cut(index)]
            send("face%d" % index)
        extra = [row_sums(total * out["direction"][...])]
        if later:
            extra.append(0.5 * row_sums(out["direction"][...] * get("before")[...]))
        totals = jnp.sum(get("arrived")[...], axis=0)
        out["totals"][...] = totals
        send("totals")
        out["block"][...] = gather_chunk(get, totals, extra)
        send("block")

    def second_residual(get, out, send):
        values, energy, sums = solve_coarse(get)
        dot = get("totals")[own : own + 1]
        curve = sums[0:1] + energy
        step = dot / curve
        out["rows"][...] = jnp.concatenate([step, curve, dot, jnp.zeros((5, count), F32)], axis=0)
        send("rows")
        scale = as_columns(step, face)
        total = None
        for index in range(6):
            product = image_face(get, index, values)
            out["image"][:, cut(index)] = product
            value = get("residual")[:, cut(index)] - scale * product
            out["second"][:, cut(index)] = value
            total = times_matrix(get, total, index, value)
        send("image")
        send("second")
        for index in range(6):
            out["face%d" % index][...] = total[:, cut(index)]
            send("face%d" % index)
        out["chunks"][...] = scatter_loads(
            get,
            total,
            lambda index: jnp.concatenate(
                [get("coupling")[:, cut(index)], get("other")[:, cut(index)]], axis=0
            ),
            get("numbers")[...],
            row_sums(total * out["second"][...]),
        )
        send("chunks")

    def finish(get, out, send):
        values, energy, sums = solve_coarse(get)
        rows = get("rows")
        first, curve, dot = rows[0:1], rows[1:2], rows[2:3]
        new_dot = get("totals")[own : own + 1]
        ratio = new_dot / dot
        step = new_dot / (sums[0:1] + energy + 2.0 * ratio * sums[1:2] + ratio * ratio * curve)
        scale = as_columns(step, face)
        ratio_columns = as_columns(ratio, face)
        earlier = as_columns(first + step * ratio, face)
        for index in range(6):
            out["multipliers"][:, cut(index)] = (
                earlier * get("first")[:, cut(index)] + scale * get("next")[:, cut(index)]
            )
        send("multipliers")
        for index in range(6):
            product = image_face(get, index, values) + ratio_columns * get("before")[:, cut(index)]
            out["last"][:, cut(index)] = get("second")[:, cut(index)] - scale * product
        send("last")

    def received_faces(arrays):
        return {"received%d" % index: value for index, value in enumerate(arrays)}

    def faces_of(result):
        return {"face%d" % index: result["face%d" % index] for index in range(6)}

    def sent_faces(result):
        return received_faces(exchange([result["face%d" % index] for index in range(6)]))

    whole = pl.BlockSpec(memory_space=pltpu.VMEM)
    scalar = pl.BlockSpec(memory_space=pltpu.SMEM)
    *opened, info = pl.pallas_call(
        opening,
        out_shape=tuple([jax.ShapeDtypeStruct((longer, face), F32)] * 6)
        + (jax.ShapeDtypeStruct((8 + corners, face), F32),),
        in_specs=[whole, whole, scalar, scalar],
        out_specs=(whole,) * 7,
        compiler_params=pltpu.CompilerParams(vmem_limit_bytes=67043328),
    )(load_terms[0], coupling, face_live, corner_ids)
    slots = face_map[0]
    fixed = dict(slots=slots, info=info)
    blocks = {"matrix": 6}
    one = run(
        start,
        dict(
            loads=load_terms[0],
            **fixed,
            **received_faces(exchange(opened)),
            coupling=coupling,
            matrix=dirichlet[0],
        ),
        dict(
            residual=field,
            **six,
            other=((terms, size), BF16),
            numbers=((named + 8, LANES), F32),
            chunks=sent_block,
        ),
        matmul_flops,
        blocks,
    )
    received = sent_faces(one)
    arrived = spread_out(one["chunks"])
    gathered_block = ((devices, gathered, count), F32)
    two = run(
        lambda get, out, send: image(get, out, send, False),
        dict(
            **fixed,
            **faces_of(one),
            **received,
            matrix=dual_operator[0],
            arrived=arrived,
            inverse=coarse_inverse,
        ),
        dict(direction=field, **six, totals=rows8, block=gathered_block),
        matmul_flops,
        blocks,
    )
    known = dict(coupling=coupling, other=one["other"], numbers=one["numbers"])
    received = sent_faces(two)
    block = spread_out(two["block"])
    three = run(
        second_residual,
        dict(
            block=block,
            totals=two["totals"],
            **fixed,
            **known,
            **faces_of(two),
            **received,
            residual=one["residual"],
            matrix=dirichlet[0],
        ),
        dict(rows=rows8, image=field, second=field, **six, chunks=sent_block),
        matmul_flops,
        blocks,
    )
    received = sent_faces(three)
    arrived = spread_out(three["chunks"])
    four = run(
        lambda get, out, send: image(get, out, send, True),
        dict(
            **fixed,
            **faces_of(three),
            **received,
            matrix=dual_operator[0],
            before=three["image"],
            arrived=arrived,
            inverse=coarse_inverse,
        ),
        dict(direction=field, **six, totals=rows8, block=gathered_block),
        matmul_flops,
        blocks,
    )
    received = sent_faces(four)
    block = spread_out(four["block"])
    five = run(
        finish,
        dict(
            block=block,
            totals=four["totals"],
            rows=three["rows"],
            **fixed,
            **known,
            first=two["direction"],
            next=four["direction"],
            **faces_of(four),
            **received,
            before=three["image"],
            second=three["second"],
        ),
        dict(multipliers=field, last=field),
    )
    return (five["multipliers"][None], five["last"][None])


def solution(mesh):
    placed = (
        P(AXES, None, None),
        P(AXES, None, None),
        P(AXES, None, None),
        P(AXES, None, None),
        P(AXES, None),
        P(AXES, None, None),
        P(AXES, None),
        P(AXES, None),
    )
    return jax.shard_map(
        local,
        mesh=mesh,
        in_specs=placed,
        out_specs=(P(AXES, None, None), P(AXES, None, None)),
        check_vma=False,
    )
```

time: 434 us -> 128 us (0.29)
  blocking collectives: 199 us -> 0 us
  local copies, waits for them, and re-layouts: 101 us -> 1.28 us
  other arithmetic: 53 us -> 0 us
  waiting for transfers between devices: 0.08 us -> 34.6 us
  Pallas kernels: 0 us -> 31.9 us
  matrix products: 23.2 us -> 0 us
  starting transfers between devices: 53.7 us -> 58.8 us
    psum x3 -> x0, blocking collectives: 116 us -> none  [the longest x2 79.2 us: local(): lax.psum((coarse_local, local_curve), ('cluster', 'sub'))]
    all_gather x2 -> x0, blocking collectives: 82.9 us -> none  [local(): lax.all_gather(own_values, ('cluster', 'sub'), axis=1, tiled=True)]
    gather x60 -> x0, local copies, waits for them, and re-layouts: 55.5 us -> none  [assemble(): permuted = jnp.take(received[face_index], slot_maps[face_index], axis=1)]
    unnamed x25 -> x0, other arithmetic: 39.7 us -> none
    ppermute x30, waiting for transfers between devices: 0.08 us -> 34.6 us  [shifted(): lax.ppermute(value, axis, [(i, (i + steps) % count) for i in range(count)])]
    pallas_call x0 -> x6, Pallas kernels: none -> 31.9 us  [the longest x5 29.8 us: run(): pl.pallas_call(kernel, out_shape=tuple((jax.ShapeDtypeStruct(*outs[name])...]
    dot_general x14 -> x0, matrix products: 23.2 us -> none  [the longest x2 8.22 us: precond_with_product(): jnp.dot(vector.astype(jnp.bfloat16), precond_local, preferred_element_typ...]
    unnamed x184 -> x1, local copies, waits for them, and re-layouts: 20.4 us -> 1.28 us
  transfers between devices with their start and end apart: 30 -> 34, of which waited for: 0 -> 15; matrix products, arithmetic and copies ran while one was open for 20% -> 1% of each run, Pallas kernels for 0% -> 0%
where the time goes in v2:
time: 128 us; the launch traced here: 127 us
  starting transfers between devices  58.8 us (46%)
  waiting for transfers between devices  34.6 us (27%)
  Pallas kernels  31.9 us (25%)
  local copies, waits for them, and re-layouts  1.28 us (1%)
    ppermute x30, starting transfers between devices, shifted(): lax.ppermute(value, axis, [(i, (i + steps) % count) for i in range(count)])  45.3 us
    ppermute x30, waiting for transfers between devices, shifted(): lax.ppermute(value, axis, [(i, (i + steps) % count) for i in range(count)])  34.6 us
    pallas_call x5, Pallas kernels, run(): pl.pallas_call(kernel, out_shape=tuple((jax.ShapeDtypeStruct(*outs[name])...  29.8 us
    all_to_all x4, starting transfers between devices, spread_out(): return lax.all_to_all(chunks, AXES, 0, 0, tiled=True)  13.5 us
  transfers between devices with their start and end apart: 34, of which 15 were waited for; matrix products, arithmetic and copies ran while one was open for 1% of the time, Pallas kernels for 0%

profile of v2, /device:TPU:0, one launch (start us, length us, event | category | flops | bytes accessed | tf_op | source)
XLA Modules:
  0.0 127.3 jit_solution(9282912124840311934)
XLA Ops:
  0.6 2.1 %shard_map.95 = (f32[160,256]{1,0:T(8,128)}, f32[160,256]{1,0:T(8,128)}, f32[160,256]{1,0:T(8,128)}, f32[160,256]{1,0:T(8,128)}, f32[160,256]{1,0:T(8,128)}, /*index=5*/f32[160,256]{1,0:T(8,128)}, f32[16,256]{1,0:T(8,128)}) custom-call(f32[128,1536]{1,0:T(8,128)} %bitcast.15, bf16[24,1536]{1,0:T(8,128)(2,1)} %bitcast.17, s32[1,6]{1,0:T(1,128)} %live_ref.1, ...), custom_call_target="tpu_custom_call" | custom-call | tf_op jit(solution)/shard_map/pallas_call | solution.py:414
  2.7 3.0 %collective-permute-start = (f32[160,256]{1,0:T(8,128)}, f32[160,256]{1,0:T(8,128)}, u32[]{:S(2)}, u32[]{:S(2)}) collective-permute-start(f32[160,256]{1,0:T(8,128)} %get-tuple-element.50), channel_id=1, source_target_pairs={{0,16},{16,0},{1,17},{17,1},{2,18},{18,2},{3,19},{19,3},{4,20},{20... | collective-permute-start | bytes 491528 | tf_op jit(solution)/shard_map/ppermute | solution.py:21
  5.8 4.4 %collective-permute-start.3 = (f32[160,256]{1,0:T(8,128)}, f32[160,256]{1,0:T(8,128)}, u32[]{:S(2)}, u32[]{:S(2)}) collective-permute-start(f32[160,256]{1,0:T(8,128)} %get-tuple-element.53), channel_id=1, source_target_pairs={{0,15},{1,0},{2,1},{3,2},{4,3},{5,4},{6,5},{7,6},{8,7},{9,8},{10,9... | collective-permute-start | bytes 491528 | tf_op jit(solution)/shard_map/ppermute | solution.py:21
  11.1 4.1 %collective-permute-start.5 = (f32[160,256]{1,0:T(8,128)}, f32[160,256]{1,0:T(8,128)}, u32[]{:S(2)}, u32[]{:S(2)}) collective-permute-start(f32[160,256]{1,0:T(8,128)} %get-tuple-element.55), channel_id=1, source_target_pairs={{0,12},{1,13},{2,14},{3,15},{4,0},{5,1},{6,2},{7,3},{8,4},{9,5},{1... | collective-permute-start | bytes 491528 | tf_op jit(solution)/shard_map/ppermute | solution.py:21
  16.5 3.3 %collective-permute-done.4.refs_7_ = f32[160,256]{1,0:T(8,128)} collective-permute-done((f32[160,256]{1,0:T(8,128)}, f32[160,256]{1,0:T(8,128)}, u32[]{:S(2)}, u32[]{:S(2)}) %collective-permute-start.4) | collective-permute-done | bytes 163872 | tf_op jit(solution)/shard_map/ppermute | solution.py:21
  21.1 6.3 %shard_map.96 = (f32[128,1536]{1,0:T(8,128)}, f32[128,256]{1,0:T(8,128)}, f32[128,256]{1,0:T(8,128)}, f32[128,256]{1,0:T(8,128)}, f32[128,256]{1,0:T(8,128)}, /*...) custom-call(f32[128,1536]{1,0:T(8,128)} %bitcast.16, ...), custom_call_target="tpu_custom_call" | custom-call | flops 603979776 | bytes 6584320 | tf_op jit(solution)/shard_map/pallas_call | solution.py:93
  29.0 3.3 %all-to-all-start = ((f32[32,8,128]{2,1,0:T(8,128)}), f32[32,8,128]{2,1,0:T(8,128)}, u32[]{:S(2)}, u32[]{:S(2)}) async-start(f32[32,8,128]{2,1,0:T(8,128)} %get-tuple-element.62), calls=%async_computation | async-start | bytes 262144 | tf_op jit(solution)/shard_map/all_to_all | solution.py:36
  33.9 3.8 %collective-permute-start.9 = (f32[128,256]{1,0:T(8,128)}, f32[128,256]{1,0:T(8,128)}, u32[]{:S(2)}, u32[]{:S(2)}) collective-permute-start(f32[128,256]{1,0:T(8,128)} %get-tuple-element.58.refs_4_), channel_id=1, source_target_pairs={{0,15},{1,0},{2,1},{3,2},{4,3},{5,4},{6,5},{7,6},{8,7},{9,8},{10,9... | collective-permute-start | bytes 393224 | tf_op jit(solution)/shard_map/ppermute | solution.py:21
  41.7 4.1 %collective-permute-done.8.refs_10_ = f32[128,256]{1,0:T(8,128)} collective-permute-done((f32[128,256]{1,0:T(8,128)}, f32[128,256]{1,0:T(8,128)}, u32[]{:S(2)}, u32[]{:S(2)}) %collective-permute-start.8) | collective-permute-done | bytes 131104 | tf_op jit(solution)/shard_map/ppermute | solution.py:21
  47.1 5.5 %shard_map.97 = (f32[128,1536]{1,0:T(8,128)}, f32[128,256]{1,0:T(8,128)}, f32[128,256]{1,0:T(8,128)}, f32[128,256]{1,0:T(8,128)}, f32[128,256]{1,0:T(8,128)}, /*...) custom-call(s32[6,256]{1,0:T(8,128)} %bitcast.22, ...), custom_call_target="tpu_custom_call" | custom-call | flops 603979776 | bytes 6446208 | tf_op jit(solution)/shard_map/pallas_call | solution.py:93
  53.2 3.4 %all-to-all-start.1 = ((f32[32,8,128]{2,1,0:T(8,128)}), f32[32,8,128]{2,1,0:T(8,128)}, u32[]{:S(2)}, u32[]{:S(2)}) async-start(f32[32,8,128]{2,1,0:T(8,128)} %get-tuple-element.63), calls=%async_computation.1 | async-start | bytes 262144 | tf_op jit(solution)/shard_map/all_to_all | solution.py:36
  58.4 3.7 %collective-permute-start.15 = (f32[128,256]{1,0:T(8,128)}, f32[128,256]{1,0:T(8,128)}, u32[]{:S(2)}, u32[]{:S(2)}) collective-permute-start(f32[128,256]{1,0:T(8,128)} %get-tuple-element.69.refs_9_), channel_id=1, source_target_pairs={{0,15},{1,0},{2,1},{3,2},{4,3},{5,4},{6,5},{7,6},{8,7},{9,8},{10,9... | collective-permute-start | bytes 393224 | tf_op jit(solution)/shard_map/ppermute | solution.py:21
  64.2 1.9 %collective-permute-done.15.refs_16_ = f32[128,256]{1,0:T(8,128)} collective-permute-done((f32[128,256]{1,0:T(8,128)}, f32[128,256]{1,0:T(8,128)}, u32[]{:S(2)}, u32[]{:S(2)}) %collective-permute-start.15) | collective-permute-done | bytes 131104 | tf_op jit(solution)/shard_map/ppermute | solution.py:21
  66.1 4.1 %collective-permute-done.14.refs_15_ = f32[128,256]{1,0:T(8,128)} collective-permute-done((f32[128,256]{1,0:T(8,128)}, f32[128,256]{1,0:T(8,128)}, u32[]{:S(2)}, u32[]{:S(2)}) %collective-permute-start.14) | collective-permute-done | bytes 131104 | tf_op jit(solution)/shard_map/ppermute | solution.py:21
  71.5 7.5 %shard_map.98 = (f32[8,128]{1,0:T(8,128)}, f32[128,1536]{1,0:T(8,128)}, f32[128,1536]{1,0:T(8,128)}, f32[128,256]{1,0:T(8,128)}, f32[128,256]{1,0:T(8,128)}, /*i...) custom-call(f32[32,8,128]{2,1,0:T(8,128)} %all-to-all-done.1.refs_0_, ...), custom_call_target="tpu_custom_call" | custom-call | flops 603979776 | bytes 7473152 | tf_op jit(solution)/shard_map/pallas_call | solution.py:93
  79.6 3.4 %all-to-all-start.2 = ((f32[32,8,128]{2,1,0:T(8,128)}), f32[32,8,128]{2,1,0:T(8,128)}, u32[]{:S(2)}, u32[]{:S(2)}) async-start(f32[32,8,128]{2,1,0:T(8,128)} %get-tuple-element.81), calls=%async_computation.2 | async-start | bytes 262144 | tf_op jit(solution)/shard_map/all_to_all | solution.py:36
  84.8 3.7 %collective-permute-start.21 = (f32[128,256]{1,0:T(8,128)}, f32[128,256]{1,0:T(8,128)}, u32[]{:S(2)}, u32[]{:S(2)}) collective-permute-start(f32[128,256]{1,0:T(8,128)} %get-tuple-element.76.refs_4_), channel_id=1, source_target_pairs={{0,15},{1,0},{2,1},{3,2},{4,3},{5,4},{6,5},{7,6},{8,7},{9,8},{10,9... | collective-permute-start | bytes 393224 | tf_op jit(solution)/shard_map/ppermute | solution.py:21
  90.5 1.9 %collective-permute-done.21.refs_11_ = f32[128,256]{1,0:T(8,128)} collective-permute-done((f32[128,256]{1,0:T(8,128)}, f32[128,256]{1,0:T(8,128)}, u32[]{:S(2)}, u32[]{:S(2)}) %collective-permute-start.21) | collective-permute-done | bytes 131104 | tf_op jit(solution)/shard_map/ppermute | solution.py:21
  92.5 4.1 %collective-permute-done.20.refs_10_ = f32[128,256]{1,0:T(8,128)} collective-permute-done((f32[128,256]{1,0:T(8,128)}, f32[128,256]{1,0:T(8,128)}, u32[]{:S(2)}, u32[]{:S(2)}) %collective-permute-start.20) | collective-permute-done | bytes 131104 | tf_op jit(solution)/shard_map/ppermute | solution.py:21
  97.9 5.6 %shard_map.99 = (f32[128,1536]{1,0:T(8,128)}, f32[128,256]{1,0:T(8,128)}, f32[128,256]{1,0:T(8,128)}, f32[128,256]{1,0:T(8,128)}, f32[128,256]{1,0:T(8,128)}, /*...) custom-call(s32[6,256]{1,0:T(8,128)} %bitcast.24, ...), custom_call_target="tpu_custom_call" | custom-call | flops 603979776 | bytes 7232640 | tf_op jit(solution)/shard_map/pallas_call | solution.py:93
  104.1 3.4 %all-to-all-start.3 = ((f32[32,8,128]{2,1,0:T(8,128)}), f32[32,8,128]{2,1,0:T(8,128)}, u32[]{:S(2)}, u32[]{:S(2)}) async-start(f32[32,8,128]{2,1,0:T(8,128)} %get-tuple-element.82), calls=%async_computation.3 | async-start | bytes 262144 | tf_op jit(solution)/shard_map/all_to_all | solution.py:36
  109.3 3.7 %collective-permute-start.27 = (f32[128,256]{1,0:T(8,128)}, f32[128,256]{1,0:T(8,128)}, u32[]{:S(2)}, u32[]{:S(2)}) collective-permute-start(f32[128,256]{1,0:T(8,128)} %get-tuple-element.89.refs_12_), channel_id=1, source_target_pairs={{0,15},{1,0},{2,1},{3,2},{4,3},{5,4},{6,5},{7,6},{8,7},{9,8},{10,9... | collective-permute-start | bytes 393224 | tf_op jit(solution)/shard_map/ppermute | solution.py:21
  117.0 4.1 %collective-permute-done.26.refs_18_ = f32[128,256]{1,0:T(8,128)} collective-permute-done((f32[128,256]{1,0:T(8,128)}, f32[128,256]{1,0:T(8,128)}, u32[]{:S(2)}, u32[]{:S(2)}) %collective-permute-start.26) | collective-permute-done | bytes 131104 | tf_op jit(solution)/shard_map/ppermute | solution.py:21
  122.4 4.9 %shard_map.100 = (f32[128,1536]{1,0:T(8,128)}, f32[128,1536]{1,0:T(8,128)}) custom-call(f32[32,8,128]{2,1,0:T(8,128)} %all-to-all-done.3.refs_0_, f32[8,128]{1,0:T(8,128)} %get-tuple-element.83.refs_1_, f32[8,128]{1,0:T(8,128)} %get-tuple-element.84.refs_2_, s32[6,256]{1,0:T(8,128)} %bitcast.25, f32[16,256]{1,0:T(8,128)} %get-tuple-element.49.refs_2_.refs_1_.refs_3_.refs_4_, ...), custom_call_target="tpu_custom_call" | custom-call | bytes 5117952 | tf_op jit(solution)/shard_map/pallas_call | solution.py:93
  (51 shorter events, 31.1 us)
Async XLA Ops:
  2.7 8.3 %collective-permute-start = (f32[160,256]{1,0:T(8,128)}, f32[160,256]{1,0:T(8,128)}, u32[]{:S(2)}, u32[]{:S(2)}) collective-permute-start(f32[160,256]{1,0:T(8,128)} %get-tuple-element.50), channel_id=1, source_target_pairs={{0,16},{16,0},{1,17},{17,1},{2,18},{18,2},{3,19},{19,3},{4,20},{20... | collective-permute-start | bytes 491528 | tf_op jit(solution)/shard_map/ppermute | solution.py:21
  5.7 10.8 %collective-permute-start.1 = (f32[160,256]{1,0:T(8,128)}, f32[160,256]{1,0:T(8,128)}, u32[]{:S(2)}, u32[]{:S(2)}) collective-permute-start(f32[160,256]{1,0:T(8,128)} %get-tuple-element.51), channel_id=1, source_target_pairs={{0,16},{16,0},{1,17},{17,1},{2,18},{18,2},{3,19},{19,3},{4,20},{20... | collective-permute-start | bytes 491528 | tf_op jit(solution)/shard_map/ppermute | solution.py:21
  5.8 10.7 %collective-permute-start.2 = (f32[160,256]{1,0:T(8,128)}, f32[160,256]{1,0:T(8,128)}, u32[]{:S(2)}, u32[]{:S(2)}) collective-permute-start(f32[160,256]{1,0:T(8,128)} %get-tuple-element.52), channel_id=1, source_target_pairs={{0,1},{1,2},{2,3},{3,4},{4,5},{5,6},{6,7},{7,8},{8,9},{9,10},{10,1... | collective-permute-start | bytes 491528 | tf_op jit(solution)/shard_map/ppermute | solution.py:21
  5.8 10.7 %collective-permute-start.3 = (f32[160,256]{1,0:T(8,128)}, f32[160,256]{1,0:T(8,128)}, u32[]{:S(2)}, u32[]{:S(2)}) collective-permute-start(f32[160,256]{1,0:T(8,128)} %get-tuple-element.53), channel_id=1, source_target_pairs={{0,15},{1,0},{2,1},{3,2},{4,3},{5,4},{6,5},{7,6},{8,7},{9,8},{10,9... | collective-permute-start | bytes 491528 | tf_op jit(solution)/shard_map/ppermute | solution.py:21
  10.2 9.6 %collective-permute-start.4 = (f32[160,256]{1,0:T(8,128)}, f32[160,256]{1,0:T(8,128)}, u32[]{:S(2)}, u32[]{:S(2)}) collective-permute-start(f32[160,256]{1,0:T(8,128)} %get-tuple-element.54), channel_id=1, source_target_pairs={{0,4},{1,5},{2,6},{3,7},{4,8},{5,9},{6,10},{7,11},{8,12},{9,13},{1... | collective-permute-start | bytes 491528 | tf_op jit(solution)/shard_map/ppermute | solution.py:21
  11.1 10.0 %collective-permute-start.5 = (f32[160,256]{1,0:T(8,128)}, f32[160,256]{1,0:T(8,128)}, u32[]{:S(2)}, u32[]{:S(2)}) collective-permute-start(f32[160,256]{1,0:T(8,128)} %get-tuple-element.55), channel_id=1, source_target_pairs={{0,12},{1,13},{2,14},{3,15},{4,0},{5,1},{6,2},{7,3},{8,4},{9,5},{1... | collective-permute-start | bytes 491528 | tf_op jit(solution)/shard_map/ppermute | solution.py:21
  27.4 10.8 %collective-permute-start.7 = (f32[128,256]{1,0:T(8,128)}, f32[128,256]{1,0:T(8,128)}, u32[]{:S(2)}, u32[]{:S(2)}) collective-permute-start(f32[128,256]{1,0:T(8,128)} %get-tuple-element.56.refs_2_), channel_id=1, source_target_pairs={{0,16},{16,0},{1,17},{17,1},{2,18},{18,2},{3,19},{19,3},{4,20},{20... | collective-permute-start | bytes 393224 | tf_op jit(solution)/shard_map/ppermute | solution.py:21
  29.0 18.1 %all-to-all-start = ((f32[32,8,128]{2,1,0:T(8,128)}), f32[32,8,128]{2,1,0:T(8,128)}, u32[]{:S(2)}, u32[]{:S(2)}) async-start(f32[32,8,128]{2,1,0:T(8,128)} %get-tuple-element.62), calls=%async_computation | async-start | bytes 262144 | tf_op jit(solution)/shard_map/all_to_all | solution.py:36
  37.7 8.1 %collective-permute-start.8 = (f32[128,256]{1,0:T(8,128)}, f32[128,256]{1,0:T(8,128)}, u32[]{:S(2)}, u32[]{:S(2)}) collective-permute-start(f32[128,256]{1,0:T(8,128)} %get-tuple-element.59.refs_5_), channel_id=1, source_target_pairs={{0,1},{1,2},{2,3},{3,4},{4,5},{5,6},{6,7},{7,8},{8,9},{9,10},{10,1... | collective-permute-start | bytes 393224 | tf_op jit(solution)/shard_map/ppermute | solution.py:21
  37.7 8.1 %collective-permute-start.11 = (f32[128,256]{1,0:T(8,128)}, f32[128,256]{1,0:T(8,128)}, u32[]{:S(2)}, u32[]{:S(2)}) collective-permute-start(f32[128,256]{1,0:T(8,128)} %get-tuple-element.60.refs_6_), channel_id=1, source_target_pairs={{0,12},{1,13},{2,14},{3,15},{4,0},{5,1},{6,2},{7,3},{8,4},{9,5},{1... | collective-permute-start | bytes 393224 | tf_op jit(solution)/shard_map/ppermute | solution.py:21
  38.2 8.9 %collective-permute-start.10 = (f32[128,256]{1,0:T(8,128)}, f32[128,256]{1,0:T(8,128)}, u32[]{:S(2)}, u32[]{:S(2)}) collective-permute-start(f32[128,256]{1,0:T(8,128)} %get-tuple-element.61.refs_7_), channel_id=1, source_target_pairs={{0,4},{1,5},{2,6},{3,7},{4,8},{5,9},{6,10},{7,11},{8,12},{9,13},{1... | collective-permute-start | bytes 393224 | tf_op jit(solution)/shard_map/ppermute | solution.py:21
  52.6 10.0 %collective-permute-start.13 = (f32[128,256]{1,0:T(8,128)}, f32[128,256]{1,0:T(8,128)}, u32[]{:S(2)}, u32[]{:S(2)}) collective-permute-start(f32[128,256]{1,0:T(8,128)} %get-tuple-element.67.refs_7_), channel_id=1, source_target_pairs={{0,16},{16,0},{1,17},{17,1},{2,18},{18,2},{3,19},{19,3},{4,20},{20... | collective-permute-start | bytes 393224 | tf_op jit(solution)/shard_map/ppermute | solution.py:21
  53.2 18.3 %all-to-all-start.1 = ((f32[32,8,128]{2,1,0:T(8,128)}), f32[32,8,128]{2,1,0:T(8,128)}, u32[]{:S(2)}, u32[]{:S(2)}) async-start(f32[32,8,128]{2,1,0:T(8,128)} %get-tuple-element.63), calls=%async_computation.1 | async-start | bytes 262144 | tf_op jit(solution)/shard_map/all_to_all | solution.py:36
  62.2 8.1 %collective-permute-start.14 = (f32[128,256]{1,0:T(8,128)}, f32[128,256]{1,0:T(8,128)}, u32[]{:S(2)}, u32[]{:S(2)}) collective-permute-start(f32[128,256]{1,0:T(8,128)} %get-tuple-element.70.refs_10_), channel_id=1, source_target_pairs={{0,1},{1,2},{2,3},{3,4},{4,5},{5,6},{6,7},{7,8},{8,9},{9,10},{10,1... | collective-permute-start | bytes 393224 | tf_op jit(solution)/shard_map/ppermute | solution.py:21
  62.2 8.1 %collective-permute-start.17 = (f32[128,256]{1,0:T(8,128)}, f32[128,256]{1,0:T(8,128)}, u32[]{:S(2)}, u32[]{:S(2)}) collective-permute-start(f32[128,256]{1,0:T(8,128)} %get-tuple-element.71.refs_11_), channel_id=1, source_target_pairs={{0,12},{1,13},{2,14},{3,15},{4,0},{5,1},{6,2},{7,3},{8,4},{9,5},{1... | collective-permute-start | bytes 393224 | tf_op jit(solution)/shard_map/ppermute | solution.py:21
  62.7 8.9 %collective-permute-start.16 = (f32[128,256]{1,0:T(8,128)}, f32[128,256]{1,0:T(8,128)}, u32[]{:S(2)}, u32[]{:S(2)}) collective-permute-start(f32[128,256]{1,0:T(8,128)} %get-tuple-element.72.refs_12_), channel_id=1, source_target_pairs={{0,4},{1,5},{2,6},{3,7},{4,8},{5,9},{6,10},{7,11},{8,12},{9,13},{1... | collective-permute-start | bytes 393224 | tf_op jit(solution)/shard_map/ppermute | solution.py:21
  79.0 10.0 %collective-permute-start.19 = (f32[128,256]{1,0:T(8,128)}, f32[128,256]{1,0:T(8,128)}, u32[]{:S(2)}, u32[]{:S(2)}) collective-permute-start(f32[128,256]{1,0:T(8,128)} %get-tuple-element.74.refs_2_), channel_id=1, source_target_pairs={{0,16},{16,0},{1,17},{17,1},{2,18},{18,2},{3,19},{19,3},{4,20},{20... | collective-permute-start | bytes 393224 | tf_op jit(solution)/shard_map/ppermute | solution.py:21
  79.6 18.3 %all-to-all-start.2 = ((f32[32,8,128]{2,1,0:T(8,128)}), f32[32,8,128]{2,1,0:T(8,128)}, u32[]{:S(2)}, u32[]{:S(2)}) async-start(f32[32,8,128]{2,1,0:T(8,128)} %get-tuple-element.81), calls=%async_computation.2 | async-start | bytes 262144 | tf_op jit(solution)/shard_map/all_to_all | solution.py:36
  88.5 8.1 %collective-permute-start.20 = (f32[128,256]{1,0:T(8,128)}, f32[128,256]{1,0:T(8,128)}, u32[]{:S(2)}, u32[]{:S(2)}) collective-permute-start(f32[128,256]{1,0:T(8,128)} %get-tuple-element.77.refs_5_), channel_id=1, source_target_pairs={{0,1},{1,2},{2,3},{3,4},{4,5},{5,6},{6,7},{7,8},{8,9},{9,10},{10,1... | collective-permute-start | bytes 393224 | tf_op jit(solution)/shard_map/ppermute | solution.py:21
  88.5 8.1 %collective-permute-start.23 = (f32[128,256]{1,0:T(8,128)}, f32[128,256]{1,0:T(8,128)}, u32[]{:S(2)}, u32[]{:S(2)}) collective-permute-start(f32[128,256]{1,0:T(8,128)} %get-tuple-element.78.refs_6_), channel_id=1, source_target_pairs={{0,12},{1,13},{2,14},{3,15},{4,0},{5,1},{6,2},{7,3},{8,4},{9,5},{1... | collective-permute-start | bytes 393224 | tf_op jit(solution)/shard_map/ppermute | solution.py:21
  89.0 8.9 %collective-permute-start.22 = (f32[128,256]{1,0:T(8,128)}, f32[128,256]{1,0:T(8,128)}, u32[]{:S(2)}, u32[]{:S(2)}) collective-permute-start(f32[128,256]{1,0:T(8,128)} %get-tuple-element.79.refs_7_), channel_id=1, source_target_pairs={{0,4},{1,5},{2,6},{3,7},{4,8},{5,9},{6,10},{7,11},{8,12},{9,13},{1... | collective-permute-start | bytes 393224 | tf_op jit(solution)/shard_map/ppermute | solution.py:21
  103.5 10.0 %collective-permute-start.25 = (f32[128,256]{1,0:T(8,128)}, f32[128,256]{1,0:T(8,128)}, u32[]{:S(2)}, u32[]{:S(2)}) collective-permute-start(f32[128,256]{1,0:T(8,128)} %get-tuple-element.87.refs_10_), channel_id=1, source_target_pairs={{0,16},{16,0},{1,17},{17,1},{2,18},{18,2},{3,19},{19,3},{4,20},{20... | collective-permute-start | bytes 393224 | tf_op jit(solution)/shard_map/ppermute | solution.py:21
  104.1 18.3 %all-to-all-start.3 = ((f32[32,8,128]{2,1,0:T(8,128)}), f32[32,8,128]{2,1,0:T(8,128)}, u32[]{:S(2)}, u32[]{:S(2)}) async-start(f32[32,8,128]{2,1,0:T(8,128)} %get-tuple-element.82), calls=%async_computation.3 | async-start | bytes 262144 | tf_op jit(solution)/shard_map/all_to_all | solution.py:36
  113.5 8.9 %collective-permute-start.28 = (f32[128,256]{1,0:T(8,128)}, f32[128,256]{1,0:T(8,128)}, u32[]{:S(2)}, u32[]{:S(2)}) collective-permute-start(f32[128,256]{1,0:T(8,128)} %get-tuple-element.92.refs_15_), channel_id=1, source_target_pairs={{0,4},{1,5},{2,6},{3,7},{4,8},{5,9},{6,10},{7,11},{8,12},{9,13},{1... | collective-permute-start | bytes 393224 | tf_op jit(solution)/shard_map/ppermute | solution.py:21
  (10 other events, 77.1 us)
